TPU v7x, 32 devices: a whole 2x2x4 slice. The times are simulated.
32 devices in a mesh: dp: 8 (over y, x, core), mp: 4 (over z).
Axes of the slice: x: 2, y: 2, z: 4, core: 2. Of those that a mesh axis runs over, the one named last changes fastest.
Arguments:
- hidden_in: bfloat16 [4, 2048, 1, 768], P(None, ('dp', 'mp')), may hold values from -6 to 6
- cotangent: bfloat16 [4, 2048, 1, 768], P(None, ('dp', 'mp')), may hold values from -6 to 6
- lengths: int32 [4, 1], replicated, may hold values from 512 to 2048, as said below
- qkv_weight: bfloat16 [3, 768, 768], P(None, 'dp', 'mp'), may hold values from -0.21875 to 0.21875
- out_weight: bfloat16 [768, 768], P('mp', 'dp'), may hold values from -6 to 6
- gate_up_weight: bfloat16 [2, 768, 3072], P(None, 'dp', 'mp'), may hold values from -0.21875 to 0.21875
- down_weight: bfloat16 [3072, 768], P('mp', 'dp'), may hold values from -0.21875 to 0.21875
- norm_gain: bfloat16 [2, 768], P(None, 'dp'), may hold values from 0.5 to 1.5
- norm_bias: bfloat16 [2, 768], P(None, 'dp'), may hold values from -1.796875 to 1.796875
Outputs:
- layer_out: bfloat16 [4, 2048, 1, 768], P(None, ('dp', 'mp'))
- input_grad: float32 [4, 2048, 1, 768], P(None, ('dp', 'mp'))
- qkv_grad: float32 [3, 768, 768], P(None, 'dp', 'mp')
- out_grad: float32 [768, 768], P('mp', 'dp')
- gate_up_grad: float32 [2, 768, 3072], P(None, 'dp', 'mp')
- down_grad: float32 [3072, 768], P('mp', 'dp')
- gain_grad: float32 [2, 768], P(None, 'dp')
- bias_grad: float32 [2, 768], P(None, 'dp')
Inputs may be any that keep to these rules, and one draw needn't show every extreme that they name: `lengths`: real slots of each sequence; one sequence has exactly 2048 and one exactly 512 in every draw.
All inputs are finite; a program needn't handle non-finite values.
Results may differ from a plain program's by a relative error of at most 0.029.
Values may be sent and summed in bfloat16 or wider, within the bound.
No kernel may reach another device: no remote copies, remote signals or barrier semaphores. Data moves between devices by JAX's collectives and lax.ppermute only.
A program may use at most 320 MiB of HBM per device.

v0:
```python
import jax
import jax.numpy as jnp
from jax import lax
from jax.sharding import PartitionSpec as P

HEAD_DIM = 64


norm_eps = 1e-12
rope_base = 1000.0
masked_score = -1e30


def rope_tables(positions, half_dim):
    exponent = jnp.arange(half_dim, dtype=jnp.float32) * (1.0 / half_dim)
    inverse = jnp.power(rope_base, -exponent)
    angles = positions[:, None] * inverse[None, :]
    return (jnp.cos(angles), jnp.sin(angles))


def rotate(vectors, cosine, sine_table):
    half_dim = vectors.shape[-1] // 2
    first_half = vectors[..., :half_dim]
    second_half = vectors[..., half_dim:]
    return jnp.concatenate(
        [
            first_half * cosine - second_half * sine_table,
            second_half * cosine + first_half * sine_table,
        ],
        axis=-1,
    )


def rotate_back(gradient, cosine, sine_table):
    half_dim = gradient.shape[-1] // 2
    first_half = gradient[..., :half_dim]
    second_half = gradient[..., half_dim:]
    return jnp.concatenate(
        [
            first_half * cosine + second_half * sine_table,
            second_half * cosine - first_half * sine_table,
        ],
        axis=-1,
    )


def normalize(residual_stream, gain_row, bias_row):
    center = residual_stream - jnp.mean(residual_stream, axis=-1, keepdims=True)
    inv_std = lax.rsqrt(jnp.mean(center * center, axis=-1, keepdims=True) + norm_eps)
    scaled = center * inv_std
    return (scaled * gain_row + bias_row, scaled, inv_std)


def normalize_back(upstream, scaled, inv_std, gain_row):
    d_scaled = upstream * gain_row
    d_stream = inv_std * (
        d_scaled
        - jnp.mean(d_scaled, axis=-1, keepdims=True)
        - scaled * jnp.mean(d_scaled * scaled, axis=-1, keepdims=True)
    )
    return (d_stream, jnp.sum(upstream * scaled, axis=(0, 1)), jnp.sum(upstream, axis=(0, 1)))


def split_heads(rows, head_dim):
    return rows.reshape(
        rows.shape[0], rows.shape[1], rows.shape[2] // head_dim, head_dim
    ).transpose(1, 2, 0, 3)


def merge_heads(heads):
    return heads.transpose(2, 0, 1, 3).reshape(
        heads.shape[2], heads.shape[0], heads.shape[1] * heads.shape[3]
    )


def score_grads(
    query_part, grad_part, lse_part, delta_part, key_part, value_part, mask_part, score_scale
):
    scores = (
        jnp.einsum("shqd,shkd->shqk", query_part, key_part, preferred_element_type=jnp.float32)
        * score_scale
    )
    prob_full = jnp.where(mask_part, jnp.exp(scores - lse_part[..., None]), 0.0)
    d_probs = jnp.einsum(
        "shqd,shkd->shqk", grad_part, value_part, preferred_element_type=jnp.float32
    )
    d_scores = (prob_full * (d_probs - delta_part[..., None]) * score_scale).astype(jnp.bfloat16)
    return (d_scores, prob_full.astype(jnp.bfloat16))


def body(
    hidden_in,
    cotangent,
    lengths,
    qkv_weight,
    out_weight,
    gate_up_weight,
    down_weight,
    norm_gain,
    norm_bias,
):
    query_key_value_matrix, output_matrix, gate_up_matrix, down_matrix, gain_rows, bias_rows = (
        lax.all_gather(qkv_weight, "dp", axis=1, tiled=True),
        lax.all_gather(out_weight, "dp", axis=1, tiled=True),
        lax.all_gather(gate_up_weight, "dp", axis=1, tiled=True),
        lax.all_gather(down_weight, "dp", axis=1, tiled=True),
        lax.all_gather(norm_gain, "dp", axis=1, tiled=True),
        lax.all_gather(norm_bias, "dp", axis=1, tiled=True),
    )
    gain_rows = gain_rows.astype(jnp.float32)
    bias_rows = bias_rows.astype(jnp.float32)
    group_size = lax.axis_size("dp")
    group_rank = lax.axis_index("dp")
    model_rank = lax.axis_index("mp")
    local_rows = hidden_in.shape[1]
    slots = local_rows * lax.axis_size("mp")
    seq_total = slots * group_size
    head_dim = HEAD_DIM
    score_scale = head_dim ** (-0.5)
    span = min(group_size, 8)
    block_keys = slots * span
    key_blocks = group_size // span
    own_first = group_rank * slots
    positions = (own_first + jnp.arange(slots, dtype=jnp.int32)).astype(jnp.float32)
    cosine, sine_table = rope_tables(positions, head_dim // 2)
    acc_qkv = jnp.zeros(query_key_value_matrix.shape, jnp.float32)
    acc_out = jnp.zeros(output_matrix.shape, jnp.float32)
    acc_gate_up = jnp.zeros(gate_up_matrix.shape, jnp.float32)
    acc_down = jnp.zeros(down_matrix.shape, jnp.float32)
    acc_gain = jnp.zeros(gain_rows.shape, jnp.float32)
    acc_bias = jnp.zeros(bias_rows.shape, jnp.float32)
    layer_rows = []
    input_rows = []
    for micro_step in range(hidden_in.shape[0]):
        x_rows, grad_rows = (
            lax.all_gather(hidden_in[micro_step], "mp", axis=0, tiled=True),
            lax.all_gather(cotangent[micro_step], "mp", axis=0, tiled=True),
        )
        seq_lengths = lengths[micro_step]

        def allowed_keys(first_row, row_count):
            key_pos = first_row + jnp.arange(row_count, dtype=jnp.int32)
            return (key_pos[None, :] < seq_lengths[:, None])[:, None, None, :]

        projected_rows = jnp.einsum(
            "rsd,cde->rsce", x_rows, query_key_value_matrix, preferred_element_type=jnp.float32
        )
        q_heads = rotate(split_heads(projected_rows[:, :, 0], head_dim), cosine, sine_table).astype(
            jnp.bfloat16
        )
        k_heads = rotate(split_heads(projected_rows[:, :, 1], head_dim), cosine, sine_table).astype(
            jnp.bfloat16
        )
        v_heads = split_heads(projected_rows[:, :, 2], head_dim).astype(jnp.bfloat16)
        head_shape = q_heads.shape
        buffer_shape = (head_shape[0], head_shape[1], seq_total, head_shape[3])
        forward_first_row = jnp.int32(0)
        run_max = jnp.full(head_shape[:3], masked_score, jnp.float32)
        key_part = lax.all_gather(k_heads, "dp", axis=2, tiled=True)
        value_part = lax.all_gather(v_heads, "dp", axis=2, tiled=True)
        forward_row_count = key_part.shape[2]
        forward_key_buffer = key_part
        forward_value_buffer = value_part
        old_max = run_max
        allowed = allowed_keys(forward_first_row, forward_row_count)
        scores = (
            jnp.einsum("shqd,shkd->shqk", q_heads, key_part, preferred_element_type=jnp.float32)
            * score_scale
        )
        scores = jnp.where(allowed, scores, masked_score)
        new_max = jnp.maximum(old_max, jnp.max(scores, axis=-1))
        weights_block = jnp.where(allowed, jnp.exp(scores - new_max[..., None]), 0.0)
        new_sum = jnp.sum(weights_block, axis=-1)
        new_acc = jnp.einsum(
            "shqk,shkd->shqd",
            weights_block.astype(jnp.bfloat16),
            value_part,
            preferred_element_type=jnp.float32,
        )
        run_max = new_max
        key_buffer = forward_key_buffer
        value_buffer = forward_value_buffer
        lse = run_max + jnp.log(new_sum)
        attended = new_acc / new_sum[..., None]
        attended_reduced = merge_heads(attended).astype(jnp.bfloat16)
        residual_branch = lax.psum(
            jnp.einsum(
                "rsf,fd->rsd", attended_reduced, output_matrix, preferred_element_type=jnp.float32
            ).astype(jnp.bfloat16),
            "mp",
        ).astype(jnp.float32)
        attention_normed, scaled_one, inv_std_one = normalize(
            x_rows.astype(jnp.float32) + residual_branch, gain_rows[0], bias_rows[0]
        )
        first_low = attention_normed.astype(jnp.bfloat16)
        gate_up_rows = jnp.einsum(
            "rsd,cdf->rscf", first_low, gate_up_matrix, preferred_element_type=jnp.float32
        )
        gate_part = gate_up_rows[:, :, 0]
        up_part = gate_up_rows[:, :, 1]
        sigmoid_gate = jax.nn.sigmoid(gate_part)
        silu_gate = gate_part * sigmoid_gate
        hidden_rows = (silu_gate * up_part).astype(jnp.bfloat16)
        feedforward_output = lax.psum(
            jnp.einsum(
                "rsf,fd->rsd", hidden_rows, down_matrix, preferred_element_type=jnp.float32
            ).astype(jnp.bfloat16),
            "mp",
        ).astype(jnp.float32)
        output, scaled_two, inv_std_two = normalize(
            attention_normed + feedforward_output, gain_rows[1], bias_rows[1]
        )
        layer_rows.append(
            lax.dynamic_slice_in_dim(output, model_rank * local_rows, local_rows, 0).astype(
                jnp.bfloat16
            )
        )
        d_z2, gain_two, bias_two = normalize_back(
            grad_rows.astype(jnp.float32), scaled_two, inv_std_two, gain_rows[1]
        )
        d_ffn = d_z2.astype(jnp.bfloat16)
        acc_down = acc_down + jnp.einsum(
            "rsf,rsd->fd", hidden_rows, d_ffn, preferred_element_type=jnp.float32
        )
        d_hidden = jnp.einsum("rsd,fd->rsf", d_ffn, down_matrix, preferred_element_type=jnp.float32)
        d_gate = d_hidden * up_part * sigmoid_gate * (1.0 + gate_part * (1.0 - sigmoid_gate))
        d_up = d_hidden * silu_gate
        d_gate_up = jnp.stack([d_gate, d_up], axis=2).astype(jnp.bfloat16)
        acc_gate_up = acc_gate_up + jnp.einsum(
            "rsd,rscf->cdf", first_low, d_gate_up, preferred_element_type=jnp.float32
        )
        d_first = (
            lax.psum(
                jnp.einsum(
                    "rscf,cdf->rsd", d_gate_up, gate_up_matrix, preferred_element_type=jnp.float32
                ).astype(jnp.bfloat16),
                "mp",
            ).astype(jnp.float32)
            + d_z2
        )
        d_z1, gain_one, bias_one = normalize_back(d_first, scaled_one, inv_std_one, gain_rows[0])
        acc_gain = acc_gain + jnp.stack([gain_one, gain_two])
        acc_bias = acc_bias + jnp.stack([bias_one, bias_two])
        d_branch = d_z1.astype(jnp.bfloat16)
        acc_out = acc_out + jnp.einsum(
            "rsf,rsd->fd", attended_reduced, d_branch, preferred_element_type=jnp.float32
        )
        d_attended = split_heads(
            jnp.einsum("rsd,fd->rsf", d_branch, output_matrix, preferred_element_type=jnp.float32),
            head_dim,
        ).astype(jnp.bfloat16)
        delta = jnp.sum(d_attended.astype(jnp.float32) * attended, axis=-1)
        zero_heads = jnp.zeros(head_shape, jnp.float32)

        def query_block(step_index, partial_sums):
            first_row = step_index * block_keys
            key_part = lax.dynamic_slice_in_dim(key_buffer, first_row, block_keys, 2)
            value_part = lax.dynamic_slice_in_dim(value_buffer, first_row, block_keys, 2)
            d_scores, prob_block = score_grads(
                q_heads,
                d_attended,
                lse,
                delta,
                key_part,
                value_part,
                allowed_keys(first_row, block_keys),
                score_scale,
            )
            d_query = partial_sums[0] + jnp.einsum(
                "shqk,shkd->shqd", d_scores, key_part, preferred_element_type=jnp.float32
            )
            key_total = lax.dynamic_update_slice_in_dim(
                partial_sums[1],
                jnp.einsum(
                    "shqk,shqd->shkd", d_scores, q_heads, preferred_element_type=jnp.float32
                ),
                first_row,
                2,
            )
            value_total = lax.dynamic_update_slice_in_dim(
                partial_sums[2],
                jnp.einsum(
                    "shqk,shqd->shkd", prob_block, d_attended, preferred_element_type=jnp.float32
                ),
                first_row,
                2,
            )
            return (d_query, key_total, value_total)

        zero_keys = jnp.zeros(buffer_shape, jnp.float32)
        d_query, key_total, value_total = lax.fori_loop(
            0, key_blocks, query_block, (zero_heads, zero_keys, zero_keys)
        )
        d_key, d_value = (
            lax.psum_scatter(key_total, "dp", scatter_dimension=2, tiled=True),
            lax.psum_scatter(value_total, "dp", scatter_dimension=2, tiled=True),
        )
        d_projected = jnp.stack(
            [
                merge_heads(rotate_back(d_query, cosine, sine_table)),
                merge_heads(rotate_back(d_key, cosine, sine_table)),
                merge_heads(d_value),
            ],
            axis=2,
        ).astype(jnp.bfloat16)
        acc_qkv = acc_qkv + jnp.einsum(
            "rsd,rsce->cde", x_rows, d_projected, preferred_element_type=jnp.float32
        )
        d_input = lax.psum_scatter(
            jnp.einsum(
                "rsce,cde->rsd",
                d_projected,
                query_key_value_matrix,
                preferred_element_type=jnp.float32,
            ).astype(jnp.bfloat16),
            "mp",
            scatter_dimension=0,
            tiled=True,
        ).astype(jnp.float32)
        input_rows.append(
            d_input + lax.dynamic_slice_in_dim(d_z1, model_rank * local_rows, local_rows, 0)
        )
    qkv_grad, out_grad, gate_up_grad, down_grad, gain_grad, bias_grad = (
        lax.psum_scatter(acc_qkv, "dp", scatter_dimension=1, tiled=True),
        lax.psum_scatter(acc_out, "dp", scatter_dimension=1, tiled=True),
        lax.psum_scatter(acc_gate_up, "dp", scatter_dimension=1, tiled=True),
        lax.psum_scatter(acc_down, "dp", scatter_dimension=1, tiled=True),
        lax.psum_scatter(acc_gain, "dp", scatter_dimension=1, tiled=True),
        lax.psum_scatter(acc_bias, "dp", scatter_dimension=1, tiled=True),
    )
    return (
        jnp.stack(layer_rows),
        jnp.stack(input_rows),
        qkv_grad,
        out_grad,
        gate_up_grad,
        down_grad,
        gain_grad,
        bias_grad,
    )


def solution(mesh):
    return jax.shard_map(
        body,
        mesh=mesh,
        in_specs=(
            P(None, ("dp", "mp"), None, None),
            P(None, ("dp", "mp"), None, None),
            P(),
            P(None, "dp", "mp"),
            P("mp", "dp"),
            P(None, "dp", "mp"),
            P("mp", "dp"),
            P(None, "dp"),
            P(None, "dp"),
        ),
        out_specs=(
            P(None, ("dp", "mp"), None, None),
            P(None, ("dp", "mp"), None, None),
            P(None, "dp", "mp"),
            P("mp", "dp"),
            P(None, "dp", "mp"),
            P("mp", "dp"),
            P(None, "dp"),
            P(None, "dp"),
        ),
        check_vma=False,
    )
```

profile of v0, /device:TPU:0, one launch (start us, length us, event | category | flops | bytes accessed | tf_op | source)
XLA Modules:
  0.0 1271.0 jit_solution(13772854294208763307)
XLA Ops:
  10.7 16.3 %all-gather.3 = bf16[1,256,1,768]{3,1,2,0:T(8,128)(2,1)S(1)} all-gather(bf16[1,64,1,768]{3,1,2,0:T(8,128)(2,1)S(1)} %get-tuple-element.260), channel_id=5, replica_groups=mesh['dp'=8,'mp'=4] {'mp'}, dimensions={1}, use_global_device_ids=true | all-gather | bytes 491520 | tf_op jit(solution)/shard_map/all_gather | solution.py:136
  45.4 15.5 %all-gather.2 = bf16[1,256,1,768]{3,1,2,0:T(8,128)(2,1)S(1)} all-gather(bf16[1,64,1,768]{3,1,2,0:T(8,128)(2,1)S(1)} %get-tuple-element.261), channel_id=4, replica_groups=mesh['dp'=8,'mp'=4] {'mp'}, dimensions={1}, use_global_device_ids=true | all-gather | bytes 491520 | tf_op jit(solution)/shard_map/all_gather | solution.py:136
  62.6 15.3 %all-gather.1 = bf16[1,256,1,768]{3,1,2,0:T(8,128)(2,1)S(1)} all-gather(bf16[1,64,1,768]{3,1,2,0:T(8,128)(2,1)S(1)} %get-tuple-element.258), channel_id=3, replica_groups=mesh['dp'=8,'mp'=4] {'mp'}, dimensions={1}, use_global_device_ids=true | all-gather | bytes 491520 | tf_op jit(solution)/shard_map/all_gather | solution.py:136
  257.0 51.1 %all-reduce.18.cloned.1.call-done = (bf16[256,1,768]{2,0,1:T(8,128)(2,1)}, bf16[256,1,768]{2,0,1:T(8,128)(2,1)}, bf16[256,1,768]{2,0,1:T(8,128)(2,1)}, bf16[256,1,768]{2,0,1:T(8,128)(2,1)}) async-done(((bf16[256,1,768]{2,0,1:T(8,128)(2,1)}, bf16[256,1,768]{2,0,1:T(8,128)(2,1)}, bf16[256,1,768]{2,0,1:T(8,128)(2,1)}, bf16[256,1,768]{2,0,1:T(8,128)(2,1)}), (bf16[256,1,768]{2,0,1:T(8,128)(2,1)}, ...) | async-done | bytes 1572880 | tf_op jit(solution)/shard_map/psum | solution.py:186
  334.7 18.8 %all-gather.4 = bf16[1,256,1,768]{3,1,2,0:T(8,128)(2,1)} all-gather(bf16[1,64,1,768]{3,1,2,0:T(8,128)(2,1)S(1)} %get-tuple-element.254), channel_id=6, replica_groups=mesh['dp'=8,'mp'=4] {'mp'}, dimensions={1}, use_global_device_ids=true | all-gather | bytes 491520 | tf_op jit(solution)/shard_map/all_gather | solution.py:137
  353.5 18.6 %all-gather.5 = bf16[1,256,1,768]{3,1,2,0:T(8,128)(2,1)} all-gather(bf16[1,64,1,768]{3,1,2,0:T(8,128)(2,1)S(1)} %get-tuple-element.255), channel_id=7, replica_groups=mesh['dp'=8,'mp'=4] {'mp'}, dimensions={1}, use_global_device_ids=true | all-gather | bytes 491520 | tf_op jit(solution)/shard_map/all_gather | solution.py:137
  372.1 17.4 %all-gather.7 = bf16[1,256,1,768]{3,1,2,0:T(8,128)(2,1)} all-gather(bf16[1,64,1,768]{3,1,2,0:T(8,128)(2,1)S(1)} %get-tuple-element.256), channel_id=9, replica_groups=mesh['dp'=8,'mp'=4] {'mp'}, dimensions={1}, use_global_device_ids=true | all-gather | bytes 491520 | tf_op jit(solution)/shard_map/all_gather | solution.py:137
  389.5 18.3 %all-gather.6 = bf16[1,256,1,768]{3,1,2,0:T(8,128)(2,1)} all-gather(bf16[1,64,1,768]{3,1,2,0:T(8,128)(2,1)S(1)} %get-tuple-element.257), channel_id=8, replica_groups=mesh['dp'=8,'mp'=4] {'mp'}, dimensions={1}, use_global_device_ids=true | all-gather | bytes 491520 | tf_op jit(solution)/shard_map/all_gather | solution.py:137
  438.0 33.7 %all-reduce.10.cloned.1.call-done = bf16[256,1,768]{2,0,1:T(8,128)(2,1)} async-done(((bf16[256,1,768]{2,0,1:T(8,128)(2,1)}), bf16[256,1,768]{2,0,1:T(8,128)(2,1)}) %all-reduce.10.cloned.1.call-update) | async-done | bytes 393232 | tf_op jit(solution)/shard_map/psum | solution.py:233
  493.3 52.4 %all-reduce.14.cloned.1.call-done = (bf16[256,1,768]{2,0,1:T(8,128)(2,1)}, bf16[256,1,768]{2,0,1:T(8,128)(2,1)}, bf16[256,1,768]{2,0,1:T(8,128)(2,1)}) async-done(((bf16[256,1,768]{2,0,1:T(8,128)(2,1)}, bf16[256,1,768]{2,0,1:T(8,128)(2,1)}, bf16[256,1,768]{2,0,1:T(8,128)(2,1)}), (bf16[256,1,768]{2,0,1:T(8,128)(2,1)}, bf16[256,1,768]{2,0,1:T(8,128)(2,1)}, ...) | async-done | bytes 1179664 | tf_op jit(solution)/shard_map/psum | solution.py:233
  687.7 33.6 %reduce-scatter.40.cloned.1.call-done = f32[1,3,256,64]{2,3,1,0:T(8,128)} async-done(((f32[1,3,2048,64]{2,3,1,0:T(8,128)}), f32[1,3,256,64]{2,3,1,0:T(8,128)}) %reduce-scatter.40.cloned.1.call-update) | async-done | bytes 196624 | tf_op jit(solution)/shard_map/reduce_scatter | solution.py:296
  729.8 32.9 %reduce-scatter.28.cloned.1.call-done = f32[1,3,256,64]{2,3,1,0:T(8,128)} async-done(((f32[1,3,2048,64]{2,3,1,0:T(8,128)}), f32[1,3,256,64]{2,3,1,0:T(8,128)}) %reduce-scatter.28.cloned.1.call-update) | async-done | bytes 196624 | tf_op jit(solution)/shard_map/reduce_scatter | solution.py:296
  763.7 40.5 %reduce-scatter.32.cloned.1.call-done = f32[1,3,256,64]{2,3,1,0:T(8,128)} async-done(((f32[1,3,2048,64]{2,3,1,0:T(8,128)}), f32[1,3,256,64]{2,3,1,0:T(8,128)}) %reduce-scatter.32.cloned.1.call-update) | async-done | bytes 196624 | tf_op jit(solution)/shard_map/reduce_scatter | solution.py:295
  804.1 41.4 %reduce-scatter.26.cloned.1.call-done = f32[1,3,256,64]{2,3,1,0:T(8,128)} async-done(((f32[1,3,2048,64]{2,3,1,0:T(8,128)}), f32[1,3,256,64]{2,3,1,0:T(8,128)}) %reduce-scatter.26.cloned.1.call-update) | async-done | bytes 196624 | tf_op jit(solution)/shard_map/reduce_scatter | solution.py:295
  848.8 38.3 %reduce-scatter.34.cloned.1.call-done = f32[1,3,256,64]{2,3,1,0:T(8,128)} async-done(((f32[1,3,2048,64]{2,3,1,0:T(8,128)}), f32[1,3,256,64]{2,3,1,0:T(8,128)}) %reduce-scatter.34.cloned.1.call-update) | async-done | bytes 196624 | tf_op jit(solution)/shard_map/reduce_scatter | solution.py:296
  925.4 35.6 %reduce-scatter.58.cloned.1.call-done = f32[96,2]{1,0:T(8,128)} async-done(((f32[768,2]{1,0:T(8,128)}), f32[96,2]{1,0:T(8,128)}) %reduce-scatter.58.cloned.1.call-update) | async-done | bytes 784
  962.4 36.5 %reduce-scatter.54.cloned.1.call-done = f32[96,192]{1,0:T(8,128)} async-done(((f32[768,192]{1,0:T(8,128)}), f32[96,192]{1,0:T(8,128)}) %reduce-scatter.54.cloned.1.call-update) | async-done | bytes 73744
  1000.6 88.0 %all-reduce.12.cloned.1.call-done = f32[2,768,768]{2,0,1:T(2,128)} async-done(((f32[2,768,768]{2,0,1:T(2,128)}), f32[2,768,768]{2,0,1:T(2,128)}) %all-reduce.12.cloned.1.call-update) | async-done | bytes 4718608
  1090.6 21.2 %reduce-scatter.48.cloned.1.call-done = bf16[64,1,768]{2,0,1:T(8,128)(2,1)} async-done(((bf16[256,1,768]{2,0,1:T(8,128)(2,1)}), bf16[64,1,768]{2,0,1:T(8,128)(2,1)}) %reduce-scatter.48.cloned.1.call-update) | async-done | bytes 98320 | tf_op jit(solution)/shard_map/reduce_scatter | solution.py:309
  1112.8 20.5 %reduce-scatter.42.cloned.1.call-done = bf16[64,1,768]{2,0,1:T(8,128)(2,1)} async-done(((bf16[256,1,768]{2,0,1:T(8,128)(2,1)}), bf16[64,1,768]{2,0,1:T(8,128)(2,1)}) %reduce-scatter.42.cloned.1.call-update) | async-done | bytes 98320 | tf_op jit(solution)/shard_map/reduce_scatter | solution.py:309
  1134.3 20.4 %reduce-scatter.30.cloned.1.call-done = bf16[64,1,768]{2,0,1:T(8,128)(2,1)} async-done(((bf16[256,1,768]{2,0,1:T(8,128)(2,1)}), bf16[64,1,768]{2,0,1:T(8,128)(2,1)}) %reduce-scatter.30.cloned.1.call-update) | async-done | bytes 98320 | tf_op jit(solution)/shard_map/reduce_scatter | solution.py:309
  1155.6 20.2 %reduce-scatter.36.cloned.1.call-done = bf16[64,1,768]{2,0,1:T(8,128)(2,1)} async-done(((bf16[256,1,768]{2,0,1:T(8,128)(2,1)}), bf16[64,1,768]{2,0,1:T(8,128)(2,1)}) %reduce-scatter.36.cloned.1.call-update) | async-done | bytes 98320 | tf_op jit(solution)/shard_map/reduce_scatter | solution.py:309
  1178.6 38.9 %reduce-scatter.52.cloned.1.call-done = f32[96,576]{1,0:T(8,128)} async-done(((f32[768,576]{1,0:T(8,128)}), f32[96,576]{1,0:T(8,128)}) %reduce-scatter.52.cloned.1.call-update) | async-done | bytes 221200
  1219.4 44.3 %reduce-scatter.50.cloned.1.call-done = f32[768,96]{0,1:T(8,128)} async-done(((f32[768,768]{0,1:T(8,128)}), f32[768,96]{0,1:T(8,128)}) %reduce-scatter.50.cloned.1.call-update) | async-done | bytes 294928 | tf_op jit(solution)/shard_map/reduce_scatter | solution.py:327
  (663 shorter events, 482.6 us)
Async XLA Ops:
  8.0 300.0 %all-reduce.18.cloned.1.call-start = ((), (), s32[]{:S(2)}) async-start(), calls=%async_computation.40 | async-start | bytes 3145728 | tf_op jit(solution)/shard_map/psum | solution.py:186
  238.3 77.7 %all-gather.13.cloned.1.call-start = ((), (), s32[]{:S(2)}) async-start(), calls=%async_computation.17 | async-start | bytes 2654208 | tf_op jit(solution)/shard_map/all_gather | solution.py:105
  238.9 83.1 %all-gather.15.cloned.1.call-start = ((), (), s32[]{:S(2)}) async-start(), calls=%async_computation.18 | async-start | bytes 1327104 | tf_op jit(solution)/shard_map/all_gather | solution.py:106
  239.5 181.4 %all-reduce.16.cloned.1.call-start = ((), (), s32[]{:S(2)}) async-start(), calls=%async_computation.39 | async-start | bytes 3145728 | tf_op jit(solution)/shard_map/psum | solution.py:204
  333.6 138.1 %all-reduce.10.cloned.1.call-start = ((), (), s32[]{:S(2)}) async-start(), calls=%async_computation.19 | async-start | bytes 786432 | tf_op jit(solution)/shard_map/psum | solution.py:233
  435.5 110.2 %all-reduce.14.cloned.1.call-start = ((), (), s32[]{:S(2)}) async-start(), calls=%async_computation.38 | async-start | bytes 2359296 | tf_op jit(solution)/shard_map/psum | solution.py:233
  489.7 184.0 %reduce-scatter.46.cloned.1.call-start = ((), (), s32[]{:S(2)}) async-start(), calls=%async_computation.30 | async-start | bytes 1769472 | tf_op jit(solution)/shard_map/reduce_scatter | solution.py:296
  558.7 116.7 %reduce-scatter.38.cloned.1.call-start = ((), (), s32[]{:S(2)}) async-start(), calls=%async_computation.26 | async-start | bytes 1769472 | tf_op jit(solution)/shard_map/reduce_scatter | solution.py:295
  572.6 107.1 %reduce-scatter.44.cloned.1.call-start = ((), (), s32[]{:S(2)}) async-start(), calls=%async_computation.29 | async-start | bytes 1769472 | tf_op jit(solution)/shard_map/reduce_scatter | solution.py:295
  581.6 139.7 %reduce-scatter.40.cloned.1.call-start = ((), (), s32[]{:S(2)}) async-start(), calls=%async_computation.27 | async-start | bytes 1769472 | tf_op jit(solution)/shard_map/reduce_scatter | solution.py:296
  586.9 175.8 %reduce-scatter.28.cloned.1.call-start = ((), (), s32[]{:S(2)}) async-start(), calls=%async_computation.21 | async-start | bytes 1769472 | tf_op jit(solution)/shard_map/reduce_scatter | solution.py:296
  594.5 209.7 %reduce-scatter.32.cloned.1.call-start = ((), (), s32[]{:S(2)}) async-start(), calls=%async_computation.23 | async-start | bytes 1769472 | tf_op jit(solution)/shard_map/reduce_scatter | solution.py:295
  604.9 240.6 %reduce-scatter.26.cloned.1.call-start = ((), (), s32[]{:S(2)}) async-start(), calls=%async_computation.20 | async-start | bytes 1769472 | tf_op jit(solution)/shard_map/reduce_scatter | solution.py:295
  613.2 273.9 %reduce-scatter.34.cloned.1.call-start = ((), (), s32[]{:S(2)}) async-start(), calls=%async_computation.24 | async-start | bytes 1769472 | tf_op jit(solution)/shard_map/reduce_scatter | solution.py:296
  618.7 305.3 %reduce-scatter.56.cloned.1.call-start = ((), (), s32[]{:S(2)}) async-start(), calls=%async_computation.35 | async-start | bytes 442368
  643.0 318.0 %reduce-scatter.58.cloned.1.call-start = ((), (), s32[]{:S(2)}) async-start(), calls=%async_computation.36 | async-start | bytes 442368
  644.1 354.9 %reduce-scatter.54.cloned.1.call-start = ((), (), s32[]{:S(2)}) async-start(), calls=%async_computation.34 | async-start | bytes 884736
  648.8 439.7 %all-reduce.12.cloned.1.call-start = ((), (), s32[]{:S(2)}) async-start(), calls=%async_computation.37 | async-start | bytes 9437184
  666.7 445.1 %reduce-scatter.48.cloned.1.call-start = ((), (), s32[]{:S(2)}) async-start(), calls=%async_computation.31 | async-start | bytes 491520 | tf_op jit(solution)/shard_map/reduce_scatter | solution.py:309
  684.5 448.7 %reduce-scatter.42.cloned.1.call-start = ((), (), s32[]{:S(2)}) async-start(), calls=%async_computation.28 | async-start | bytes 491520 | tf_op jit(solution)/shard_map/reduce_scatter | solution.py:309
  725.9 428.7 %reduce-scatter.30.cloned.1.call-start = ((), (), s32[]{:S(2)}) async-start(), calls=%async_computation.22 | async-start | bytes 491520 | tf_op jit(solution)/shard_map/reduce_scatter | solution.py:309
  848.8 327.1 %reduce-scatter.36.cloned.1.call-start = ((), (), s32[]{:S(2)}) async-start(), calls=%async_computation.25 | async-start | bytes 491520 | tf_op jit(solution)/shard_map/reduce_scatter | solution.py:309
  890.8 326.7 %reduce-scatter.52.cloned.1.call-start = ((), (), s32[]{:S(2)}) async-start(), calls=%async_computation.33 | async-start | bytes 2211840
  902.1 361.6 %reduce-scatter.50.cloned.1.call-start = ((), (), s32[]{:S(2)}) async-start(), calls=%async_computation.32 | async-start | bytes 2654208 | tf_op jit(solution)/shard_map/reduce_scatter | solution.py:327
  (184 other events, 3389.3 us)
Sparse Core Ops, SparseCore 0:
  238.4 69.5 all-reduce.17
  333.7 87.1 all-reduce.15
  435.6 36.0 all-reduce.9
  489.8 55.7 all-reduce.13
Sparse Core Ops, SparseCore 1:
  240.7 29.2 all-gather.12
  271.7 23.8 all-gather.14
  558.8 37.6 reduce-scatter.45
  599.8 38.3 reduce-scatter.37
  641.4 38.2 reduce-scatter.43
  683.0 38.3 reduce-scatter.39
  724.4 38.2 reduce-scatter.27
  765.9 38.2 reduce-scatter.31
  807.3 38.2 reduce-scatter.25
  848.9 38.2 reduce-scatter.33
  890.0 33.9 reduce-scatter.55
  927.1 33.9 reduce-scatter.57
  964.0 34.9 reduce-scatter.53
  1002.3 86.3 all-reduce.11
  1090.9 20.8 reduce-scatter.47
  1114.1 19.1 reduce-scatter.41
  1135.6 19.0 reduce-scatter.29
  1156.9 18.8 reduce-scatter.35
  1179.1 38.4 reduce-scatter.51
  1221.5 42.2 reduce-scatter.49
where the time goes:
time: 1280 us; the launch traced here: 1270 us
  waiting for transfers between devices  679 us (53%)
  blocking collectives  278 us (22%)
  matrix products  154 us (12%)
  other arithmetic  74.6 us (6%)
  local copies, waits for them, and re-layouts  64.9 us (5%)
  between operations  18.9 us (1%)
    unnamed x29, waiting for transfers between devices  212 us
    reduce_scatter x4, waiting for transfers between devices, body(): lax.psum_scatter(value_total, 'dp', scatter_dimension=2, tiled=True)  105 us
    reduce_scatter x4, waiting for transfers between devices, body(): lax.psum_scatter(key_total, 'dp', scatter_dimension=2, tiled=True)  86.2 us
    psum x2, waiting for transfers between devices, body(): lax.psum(jnp.einsum('rscf,cdf->rsd', d_gate_up, gate_up_matrix, preferred...  86.1 us
    reduce_scatter x4, waiting for transfers between devices, body(): lax.psum_scatter(jnp.einsum('rsce,cde->rsd', d_projected, query_key_value...  82.2 us
    all_gather x4, blocking collectives, body(): lax.all_gather(cotangent[micro_step], 'mp', axis=0, tiled=True)  73.1 us
    all_gather x4, blocking collectives, body(): lax.all_gather(hidden_in[micro_step], 'mp', axis=0, tiled=True)  61.8 us
    all_gather x4, blocking collectives, body(): value_part = lax.all_gather(v_heads, 'dp', axis=2, tiled=True)  52.4 us
  transfers between devices with their start and end apart: 24, of which 20 were waited for; matrix products, arithmetic and copies ran while one was open for 15% of the time, Pallas kernels for 0%

commit v1 on v0

--- a/solution.py
+++ b/solution.py
@@ -1,14 +1,854 @@
+import functools
+
 import jax
 import jax.numpy as jnp
 from jax import lax
+from jax.experimental import pallas as pl
+from jax.experimental.pallas import tpu as pltpu
 from jax.sharding import PartitionSpec as P
 
 HEAD_DIM = 64
-
 
 norm_eps = 1e-12
 rope_base = 1000.0
 masked_score = -1e30
+
+BF = jnp.bfloat16
+F32 = jnp.float32
+LANES = 128
+
+CORE, XBIT, YBIT = 1, 2, 4
+PIECE = (0, XBIT, YBIT, XBIT | YBIT)
+PIECES = PIECE + tuple(j | CORE for j in PIECE)
+
+
+def swap(value, dp_mask=0, mp_mask=0):
+    mp = lax.axis_size("mp")
+    count = lax.axis_size("dp") * mp
+    mask = dp_mask * mp + mp_mask
+    return lax.ppermute(value, ("dp", "mp"), [(i, i ^ mask) for i in range(count)])
+
+
+def add_low(a, b):
+    return (a.astype(F32) + b.astype(F32)).astype(BF)
+
+
+def add_wide(a, b):
+    return a.astype(F32) + b.astype(F32)
+
+
+def gather_plane(own):
+    half = own.shape[0] // 2
+    from_x = swap(own, XBIT)
+    from_y = swap(own, YBIT)
+    low = swap(from_x[:half], YBIT)
+    high = swap(from_y[half:], XBIT)
+    mine = [own, from_x, from_y, low, high]
+    return mine + [swap(piece, CORE) for piece in mine]
+
+
+def gather_mp(block):
+    return jnp.stack([block] + [swap(block, 0, j) for j in range(1, lax.axis_size("mp"))])
+
+
+def scatter_plane(keep, send, first, second):
+    back = swap(send, CORE)
+    outgoing = add_low(keep[2:], back[2:])
+    staying = add_low(keep[:2], back[:2])
+    back = swap(outgoing, first)
+    outgoing = add_low(staying[1], back[1])
+    own = add_wide(staying[0], back[0])
+    return own + swap(outgoing, second).astype(F32)
+
+
+def order_of(first, second):
+    return (0, second, first, first | second)
+
+
+X_FIRST = order_of(XBIT, YBIT)
+Y_FIRST = order_of(YBIT, XBIT)
+
+
+def params(limit=60 << 20):
+    return pltpu.CompilerParams(vmem_limit_bytes=limit)
+
+
+def cost(flops, size):
+    return pl.CostEstimate(flops=int(flops), bytes_accessed=int(size), transcendentals=0)
+
+
+ANY = pl.BlockSpec(memory_space=pl.ANY)
+VM = pl.BlockSpec(memory_space=pltpu.VMEM)
+
+
+def dot(a, b):
+    return lax.dot_general(a, b, (((1,), (0,)), ((), ())), preferred_element_type=F32)
+
+
+def dot_t(a, b):
+    return lax.dot_general(a, b, (((1,), (1,)), ((), ())), preferred_element_type=F32)
+
+
+def dot_rows(a, b):
+    return lax.dot_general(a, b, (((0,), (0,)), ((), ())), preferred_element_type=F32)
+
+
+def piece_copies(pieces, buffer, sems, plane):
+    mine = lax.axis_index("dp")
+    copies = []
+    for side in range(2):
+        a, b, c, low, high = pieces[5 * side : 5 * side + 5]
+        half = low.shape[0]
+        tail = low.at[plane] if plane < half else high.at[plane - half]
+        for k, source in enumerate((a.at[plane], b.at[plane], c.at[plane], tail)):
+            rel = PIECE[k] | (CORE if side else 0)
+            rows = source.shape[0]
+            start = pl.multiple_of((mine ^ rel) * rows, rows)
+            copies.append(
+                pltpu.make_async_copy(
+                    source, buffer.at[pl.ds(start, rows), :], sems.at[4 * side + k]
+                )
+            )
+    return copies
+
+
+def out_copies(buffer, keep, send, order, sems, rows):
+    mine = lax.axis_index("dp")
+    copies = []
+    for i, rel in enumerate(order):
+        for side, target in enumerate((keep, send)):
+            start = pl.multiple_of((mine ^ rel ^ side) * rows, rows)
+            copies.append(
+                pltpu.make_async_copy(
+                    buffer.at[pl.ds(start, rows), :], target(i), sems.at[2 * i + side]
+                )
+            )
+    return copies
+
+
+def start_all(copies):
+    for copy in copies:
+        copy.start()
+
+
+def wait_all(copies):
+    for copy in copies:
+        copy.wait()
+
+
+def partner(u):
+    lane = lax.broadcasted_iota(jnp.int32, u.shape, 1)
+    quarter = HEAD_DIM // 2
+    return jnp.where(
+        lane % HEAD_DIM < quarter,
+        pltpu.roll(u, LANES - quarter, 1),
+        pltpu.roll(u, quarter, 1),
+    )
+
+
+def low_lanes(shape):
+    return lax.broadcasted_iota(jnp.int32, shape, 1) < HEAD_DIM
+
+
+def kv_kernel(planes, x_ref, tab_ref, *refs):
+    pieces, (kv_ref, w, sems) = refs[:10], refs[10:]
+    copies = [piece_copies(pieces, w.at[p], sems.at[p], p) for p in range(planes)]
+    for group in copies:
+        start_all(group)
+    x = x_ref[...]
+    for p in range(planes):
+        wait_all(copies[p])
+        y = dot(x, w[p])
+        y0, y1, y2 = y[:, :LANES], y[:, LANES : 2 * LANES], y[:, 2 * LANES :]
+        base = p * 3 * LANES
+        kv_ref[:, base : base + LANES] = (y0 * tab_ref[0] + partner(y0) * tab_ref[1]).astype(BF)
+        kv_ref[:, base + LANES : base + 2 * LANES] = (
+            y1 * tab_ref[2] + partner(y1) * tab_ref[3]
+        ).astype(BF)
+        kv_ref[:, base + 2 * LANES : base + 3 * LANES] = y2.astype(BF)
+
+
+def q_kernel(planes, scale, x_ref, tab_ref, *refs):
+    pieces, (q_ref, w, sems) = refs[:10], refs[10:]
+    copies = [piece_copies(pieces, w.at[p], sems.at[p], p) for p in range(planes)]
+    for group in copies:
+        start_all(group)
+    x = x_ref[...]
+    for p in range(planes):
+        wait_all(copies[p])
+        y = dot(x, w[p][:, : 2 * LANES])
+        y0, y1 = y[:, :LANES], y[:, LANES:]
+        low = low_lanes(y1.shape)
+        base = p * 2 * LANES
+        q0 = y0 * tab_ref[0] + partner(y0) * tab_ref[1]
+        q1 = jnp.where(low, y1 * tab_ref[2] + partner(y1) * tab_ref[3], 0.0)
+        q_ref[:, base : base + LANES] = (q0 * scale).astype(BF)
+        q_ref[:, base + LANES : base + 2 * LANES] = (q1 * scale).astype(BF)
+
+
+def attend_kernel(q_ref, bias_ref, *refs):
+    pieces = refs[:10]
+    att_ref, low_ref, lse_ref, s_ref = refs[10:]
+    rows = q_ref.shape[0]
+    keys = rows
+
+    def block(k, column):
+        side, index = divmod(k, 4)
+        lanes = slice(column * LANES, (column + 1) * LANES)
+        if index < 3:
+            return pieces[5 * side + index][:, lanes]
+        return jnp.concatenate(
+            [pieces[5 * side + 3][:, lanes], pieces[5 * side + 4][:, lanes]], axis=0
+        )
+
+    low = low_lanes((rows, LANES))
+    lane = lax.broadcasted_iota(jnp.int32, (rows, LANES), 1)
+    q0, q1 = q_ref[:, :LANES], q_ref[:, LANES:]
+    zero = jnp.zeros_like(q0)
+    heads = (
+        (jnp.where(low, q0, zero), 0, 2),
+        (jnp.where(low, zero, q0), 0, 2),
+        (q1, 1, 1),
+    )
+    stats = jnp.zeros((rows, LANES), F32)
+    results = []
+    for h, (q, key_column, value_column) in enumerate(heads):
+        peak = jnp.full((rows, LANES), -jnp.inf, F32)
+        for k in range(8):
+            s = dot_t(q, block(k, key_column)) + bias_ref[k : k + 1, :]
+            s_ref[:, k * keys : (k + 1) * keys] = s
+            for c in range(keys // LANES):
+                peak = jnp.maximum(peak, s[:, c * LANES : (c + 1) * LANES])
+        top = jnp.max(peak, axis=1, keepdims=True)
+        total = jnp.zeros((rows, LANES), F32)
+        acc = jnp.zeros((rows, LANES), F32)
+        for k in range(8):
+            e = jnp.exp(s_ref[:, k * keys : (k + 1) * keys] - top)
+            for c in range(keys // LANES):
+                total = total + e[:, c * LANES : (c + 1) * LANES]
+            acc = acc + dot(e.astype(BF), block(k, value_column))
+        total = jnp.sum(total, axis=1, keepdims=True)
+        results.append(acc / total)
+        stats = jnp.where(lane == h, top + jnp.log(total), stats)
+    pair = jnp.where(low, results[0], results[1])
+    single = jnp.where(low, 0.0, results[2])
+    att_ref[:, :LANES] = single
+    att_ref[:, LANES:] = pair
+    low_ref[:, :LANES] = single.astype(BF)
+    low_ref[:, LANES:] = pair.astype(BF)
+    lse_ref[0] = stats.T[:8, :]
+
+
+def attend_back_kernel(
+    order, scale, q_ref, dat_ref, lse_ref, delta_ref, bias_ref, tab_ref, *refs
+):
+    pieces = refs[:10]
+    keep_ref, send_ref, dq_ref = refs[10:]
+    rows = q_ref.shape[0]
+
+    def block(k, column):
+        side, index = divmod(k, 4)
+        lanes = slice(column * LANES, (column + 1) * LANES)
+        if index < 3:
+            return pieces[5 * side + index][:, lanes]
+        return jnp.concatenate(
+            [pieces[5 * side + 3][:, lanes], pieces[5 * side + 4][:, lanes]], axis=0
+        )
+
+    low = low_lanes((rows, LANES))
+    q0, q1 = q_ref[:, :LANES], q_ref[:, LANES:]
+    d0, d1 = dat_ref[:, LANES:], dat_ref[:, :LANES]
+    zero = jnp.zeros_like(q0)
+    heads = (
+        (jnp.where(low, q0, zero), jnp.where(low, d0, zero), 0, 2),
+        (jnp.where(low, zero, q0), jnp.where(low, zero, d0), 0, 2),
+        (q1, d1, 1, 1),
+    )
+    dq = [jnp.zeros((LANES, rows), F32) for _ in heads]
+    for k in range(8):
+        side, index = divmod(k, 4)
+        target = (keep_ref, send_ref)[side]
+        slot = order.index(PIECE[index])
+        mask = bias_ref[:, k : k + 1]
+        blocks = [block(k, c) for c in range(3)]
+        keys_t = [blocks[0].T, blocks[1].T]
+        parts = []
+        for h, (q, d, key_column, value_column) in enumerate(heads):
+            s = dot_t(blocks[key_column], q) + mask
+            dp = dot_t(blocks[value_column], d)
+            p = jnp.exp(s - lse_ref[0, h : h + 1, :])
+            ds = (p * (dp - delta_ref[0, h : h + 1, :])).astype(BF)
+            p = p.astype(BF)
+            parts.append((dot(ds, q), dot(p, d)))
+            dq[h] = dq[h] + dot(keys_t[key_column], ds)
+        target[slot, :, :LANES] = (parts[0][0] + parts[1][0]).astype(BF)
+        target[slot, :, LANES : 2 * LANES] = (parts[2][0] + parts[2][1]).astype(BF)
+        target[slot, :, 2 * LANES :] = (parts[0][1] + parts[1][1]).astype(BF)
+    row = lax.broadcasted_iota(jnp.int32, (LANES, rows), 0) < HEAD_DIM
+    pair = jnp.where(row, dq[0], dq[1]).T * scale
+    single = jnp.where(row, dq[2], 0.0).T * scale
+    dq_ref[:, :LANES] = (pair * tab_ref[0] - partner(pair) * tab_ref[1]).astype(BF)
+    dq_ref[:, LANES:] = (single * tab_ref[2] - partner(single) * tab_ref[3]).astype(BF)
+
+
+def center_scale(rows):
+    center = rows - jnp.mean(rows, axis=-1, keepdims=True)
+    inv = lax.rsqrt(jnp.mean(center * center, axis=-1, keepdims=True) + norm_eps)
+    return center * inv, inv
+
+
+def norm_back(e, scaled, inv):
+    return inv * (
+        e
+        - jnp.mean(e, axis=-1, keepdims=True)
+        - scaled * jnp.mean(e * scaled, axis=-1, keepdims=True)
+    )
+
+
+def rows_sum(value):
+    return jnp.sum(value, axis=0, keepdims=True)
+
+
+def forward_kernel(planes, x_ref, cot_ref, att_ref, norm_ref, *refs):
+    proj, wide = refs[:10], refs[10:20]
+    (
+        out_ref,
+        dz2_ref,
+        dffn_ref,
+        flow_ref,
+        scaled_ref,
+        inv_ref,
+        sums_ref,
+        gate_ref,
+        up_ref,
+        wo,
+        wf,
+        hold,
+        wo_sems,
+        wf_sems,
+        hold_sems,
+    ) = refs[20:]
+    wo_copies = [piece_copies(proj, wo.at[p], wo_sems.at[p], p) for p in range(planes)]
+    wf_copies = [piece_copies(wide, wf.at[p], wf_sems.at[p], p) for p in range(planes)]
+    for group in wo_copies + wf_copies:
+        start_all(group)
+    branch = jnp.zeros(x_ref.shape, F32)
+    for p in range(planes):
+        wait_all(wo_copies[p])
+        branch = branch + dot_t(
+            att_ref[:, p * 2 * LANES : (p + 1) * 2 * LANES], wo[p][:, LANES : 3 * LANES]
+        )
+    gain, bias = norm_ref[0:2, :], norm_ref[2:4, :]
+    scaled, inv = center_scale(x_ref[...].astype(F32) + branch)
+    scaled_ref[...] = scaled
+    inv_ref[...] = jnp.broadcast_to(inv, inv_ref.shape)
+    first = scaled * gain[0:1] + bias[0:1]
+    flow = first.astype(BF)
+    flow_ref[...] = flow
+    ffn = jnp.zeros(x_ref.shape, F32)
+    width = wf.shape[2] // 3
+    saves = []
+    for p in range(planes):
+        wait_all(wf_copies[p])
+        gate = dot(flow, wf[p][:, :width])
+        up = dot(flow, wf[p][:, width : 2 * width])
+        hold[p, 0] = gate
+        hold[p, 1] = up
+        for k, target in enumerate((gate_ref, up_ref)):
+            copy = pltpu.make_async_copy(hold.at[p, k], target.at[p], hold_sems.at[p, k])
+            copy.start()
+            saves.append(copy)
+        hidden = (gate * jax.nn.sigmoid(gate) * up).astype(BF)
+        ffn = ffn + dot_t(hidden, wf[p][:, 2 * width :])
+    scaled, inv = center_scale(first + ffn)
+    out_ref[...] = (scaled * gain[1:2] + bias[1:2]).astype(BF)
+    cot = cot_ref[...].astype(F32)
+    dz2 = norm_back(cot * gain[1:2], scaled, inv)
+    dz2_ref[...] = dz2
+    dffn_ref[...] = dz2.astype(BF)
+    sums_ref[...] = jnp.concatenate(
+        [rows_sum(cot * scaled), rows_sum(cot), jnp.zeros((6, cot.shape[1]), F32)], axis=0
+    )
+    wait_all(saves)
+
+
+def ffn_back_kernel(plane, order, rows, acc_ref, flow_ref, dffn_ref, gate_ref, up_ref, *refs):
+    wide = refs[:10]
+    dfirst_ref, keep_ref, send_ref, wf, grads, wf_sems, out_sems = refs[10:]
+    copies = piece_copies(wide, wf, wf_sems, plane)
+    start_all(copies)
+    gate, up = gate_ref[0], up_ref[0]
+    sig = jax.nn.sigmoid(gate)
+    silu = gate * sig
+    hidden = (silu * up).astype(BF)
+    width = gate.shape[1]
+    flow_t = flow_ref[...].T
+    dffn = dffn_ref[...]
+    grads[2] = dot(dffn.T, hidden).astype(BF)
+    outs = []
+
+    def emit(k):
+        lanes = slice(k * width, (k + 1) * width)
+        group = out_copies(
+            grads.at[k],
+            lambda i: keep_ref.at[i, :, lanes],
+            lambda i: send_ref.at[i, :, lanes],
+            order,
+            out_sems.at[k],
+            rows,
+        )
+        start_all(group)
+        outs.extend(group)
+
+    emit(2)
+    wait_all(copies)
+    d_hidden = dot(dffn, wf[:, 2 * width :])
+    d_up = (d_hidden * silu).astype(BF)
+    d_gate = (d_hidden * up * sig * (1.0 + gate * (1.0 - sig))).astype(BF)
+    grads[0] = dot(flow_t, d_gate).astype(BF)
+    emit(0)
+    grads[1] = dot(flow_t, d_up).astype(BF)
+    emit(1)
+    dfirst_ref[...] = (
+        acc_ref[...] + dot_t(d_gate, wf[:, :width]) + dot_t(d_up, wf[:, width : 2 * width])
+    )
+    wait_all(outs)
+
+
+def branch_back_kernel(
+    planes, rows, dfirst_ref, scaled_ref, inv_ref, norm_ref, att_ref, att_low_ref, *refs
+):
+    proj = refs[:10]
+    (
+        dz1_ref,
+        dat_ref,
+        delta_ref,
+        sums_ref,
+        keep_x,
+        send_x,
+        keep_y,
+        send_y,
+        wo,
+        grads,
+        wo_sems,
+        out_sems,
+    ) = refs[10:]
+    copies = [piece_copies(proj, wo.at[p], wo_sems.at[p], p) for p in range(planes)]
+    for group in copies:
+        start_all(group)
+    dfirst = dfirst_ref[...]
+    scaled = scaled_ref[...]
+    sums_ref[...] = jnp.concatenate(
+        [rows_sum(dfirst * scaled), rows_sum(dfirst), jnp.zeros((6, dfirst.shape[1]), F32)], axis=0
+    )
+    dz1 = norm_back(dfirst * norm_ref[0:1, :], scaled, inv_ref[:, 0:1])
+    dz1_ref[...] = dz1
+    d_branch = dz1.astype(BF)
+    branch_t = d_branch.T
+    outs = []
+    half = planes // 2
+    low = low_lanes((dfirst.shape[0], LANES))
+    lane = lax.broadcasted_iota(jnp.int32, (dfirst.shape[0], LANES), 1)
+    for p in range(planes):
+        lanes = slice(p * 2 * LANES, (p + 1) * 2 * LANES)
+        grads[p] = dot(branch_t, att_low_ref[:, lanes]).astype(BF)
+        keep, send, order = (keep_x, send_x, X_FIRST) if p < half else (keep_y, send_y, Y_FIRST)
+        group = out_copies(
+            grads.at[p],
+            lambda i: keep.at[i, p % half],
+            lambda i: send.at[i, p % half],
+            order,
+            out_sems.at[p],
+            rows,
+        )
+        start_all(group)
+        outs.extend(group)
+        wait_all(copies[p])
+        d = dot(d_branch, wo[p][:, LANES : 3 * LANES])
+        single = jnp.where(low, 0.0, d[:, :LANES]).astype(BF)
+        pair = d[:, LANES:].astype(BF)
+        dat_ref[:, p * 2 * LANES : p * 2 * LANES + LANES] = single
+        dat_ref[:, p * 2 * LANES + LANES : (p + 1) * 2 * LANES] = pair
+        both = pair.astype(F32) * att_ref[:, p * 2 * LANES + LANES : (p + 1) * 2 * LANES]
+        alone = single.astype(F32) * att_ref[:, p * 2 * LANES : p * 2 * LANES + LANES]
+        zero = jnp.zeros_like(both)
+        stats = zero
+        for h, part in enumerate((jnp.where(low, both, zero), jnp.where(low, zero, both), alone)):
+            stats = jnp.where(lane == h, jnp.sum(part, axis=1, keepdims=True), stats)
+        delta_ref[p] = stats.T[:8, :]
+    wait_all(outs)
+
+
+def project_back_kernel(planes, columns, used, rows, mode, x_ref, d_ref, acc_ref, tab_ref, *refs):
+    pieces = refs[:10]
+    din_ref, keep_x, send_x, keep_y, send_y, w, grads, w_sems, out_sems = refs[10:]
+    copies = [piece_copies(pieces, w.at[p], w_sems.at[p], p) for p in range(planes)]
+    for group in copies:
+        start_all(group)
+    x_t = x_ref[...].T
+    total = acc_ref[...]
+    outs = []
+    half = planes // 2
+    for p in range(planes):
+        base = p * used
+        if mode:
+            d0 = d_ref[:, base : base + LANES].astype(F32)
+            d1 = d_ref[:, base + LANES : base + 2 * LANES].astype(F32)
+            d2 = d_ref[:, base + 2 * LANES : base + 3 * LANES].astype(F32)
+            d = jnp.concatenate(
+                [
+                    (d0 * tab_ref[0] - partner(d0) * tab_ref[1]).astype(BF),
+                    (d1 * tab_ref[2] - partner(d1) * tab_ref[3]).astype(BF),
+                    d2.astype(BF),
+                ],
+                axis=1,
+            )
+        else:
+            d = d_ref[:, base : base + used]
+        grads[p] = dot(x_t, d).astype(BF)
+        keep, send, order = (keep_x, send_x, X_FIRST) if p < half else (keep_y, send_y, Y_FIRST)
+        group = out_copies(
+            grads.at[p],
+            lambda i: keep.at[i, p % half],
+            lambda i: send.at[i, p % half],
+            order,
+            out_sems.at[p],
+            rows,
+        )
+        start_all(group)
+        outs.extend(group)
+        wait_all(copies[p])
+        total = total + dot_t(d, w[p][:, :used])
+    din_ref[...] = total.astype(din_ref.dtype)
+    wait_all(outs)
+
+
+def sds(shape, dtype):
+    return jax.ShapeDtypeStruct(shape, dtype)
+
+
+def plane_body(
+    hidden_in,
+    cotangent,
+    lengths,
+    qkv_weight,
+    out_weight,
+    gate_up_weight,
+    down_weight,
+    norm_gain,
+    norm_bias,
+):
+    planes = lax.axis_size("mp")
+    group = lax.axis_size("dp")
+    dp, mp = lax.axis_index("dp"), lax.axis_index("mp")
+    part = hidden_in.shape[1]
+    width = hidden_in.shape[3]
+    rows = part * planes
+    slab = qkv_weight.shape[1]
+    ff = gate_up_weight.shape[2]
+    scale = HEAD_DIM ** (-0.5)
+    mine = mp ^ jnp.arange(planes, dtype=jnp.int32)
+
+    def exchange_in(array):
+        array = array.reshape(array.shape[0], part, width)
+        blocks = [lax.dynamic_index_in_dim(array, mine[j], 0, keepdims=False) for j in range(planes)]
+        return [blocks[0]] + [swap(blocks[j], 0, j) for j in range(1, planes)]
+
+    def exchange_out(blocks):
+        got = jnp.stack([blocks[0]] + [swap(blocks[j], 0, j) for j in range(1, planes)])
+        return jnp.stack(
+            [lax.dynamic_index_in_dim(got, mine[m], 0, keepdims=False) for m in range(planes)]
+        )
+
+    q_w, k_w, v_w = qkv_weight[0], qkv_weight[1], qkv_weight[2]
+    o_w = out_weight.T
+    two = 2 * HEAD_DIM
+    kv_own = jnp.concatenate([k_w[:, :two], k_w[:, two:], v_w[:, two:], v_w[:, :two]], axis=1)
+    qo_own = jnp.concatenate([q_w[:, :two], q_w[:, two:], o_w[:, two:], o_w[:, :two]], axis=1)
+    ffn_own = jnp.concatenate([gate_up_weight[0], gate_up_weight[1], down_weight.T], axis=1)
+
+    x_parts = exchange_in(hidden_in)
+    kv_w = gather_plane(gather_mp(kv_own))
+    x = jnp.concatenate(x_parts, axis=0)
+    qo_w = gather_plane(gather_mp(qo_own))
+    ffn_w = gather_plane(gather_mp(ffn_own))
+    cot = jnp.concatenate(exchange_in(cotangent), axis=0)
+
+    norm_own = jnp.concatenate([norm_gain, norm_bias, jnp.zeros((4, slab), BF)], axis=0)
+    norms = lax.dynamic_update_slice(
+        jnp.zeros((8, width), F32), norm_own.astype(F32), (0, dp * slab)
+    )
+    for mask in (CORE, XBIT, YBIT):
+        norms = norms + swap(norms, mask)
+
+    within = (mine[:, None] * part + jnp.arange(part, dtype=jnp.int32)[None, :]).reshape(rows)
+    positions = (dp * rows + within).astype(F32)
+    half = HEAD_DIM // 2
+    exponent = jnp.arange(half, dtype=F32) * (1.0 / half)
+    angles = positions[:, None] * jnp.power(rope_base, -exponent)[None, :]
+    cosine, sine = jnp.cos(angles), jnp.sin(angles)
+    cos_head = jnp.concatenate([cosine, cosine], axis=1)
+    sin_head = jnp.concatenate([-sine, sine], axis=1)
+    one, none = jnp.ones_like(cos_head), jnp.zeros_like(cos_head)
+    cat = lambda a, b: jnp.concatenate([a, b], axis=1)
+    tables = jnp.stack(
+        [cat(cos_head, cos_head), cat(sin_head, sin_head), cat(cos_head, one), cat(sin_head, none)]
+    )
+    length = lax.dynamic_index_in_dim(lengths.reshape(-1), mp, 0, keepdims=False)
+    piece_base = (dp ^ jnp.array(PIECES, dtype=jnp.int32)) * rows
+    key_pos = piece_base[:, None] + within[None, :]
+    bias = jnp.where(key_pos < length, 0.0, masked_score).astype(F32)
+    bias_t = bias.T
+
+    w_size = planes * group * slab * 3 * LANES * 2
+    dma = pltpu.SemaphoreType.DMA
+    kv = pl.pallas_call(
+        functools.partial(kv_kernel, planes),
+        out_shape=sds((rows, planes * 3 * LANES), BF),
+        in_specs=[VM, VM] + [ANY] * 10,
+        out_specs=VM,
+        scratch_shapes=[pltpu.VMEM((planes, width, 3 * LANES), BF), dma((planes, 8))],
+        compiler_params=params(),
+        cost_estimate=cost(2 * rows * width * planes * 3 * LANES, w_size),
+        name="kv_project",
+    )(x, tables, *kv_w)
+
+    split = rows // 2
+    kv_x, kv_y = swap(kv, XBIT), swap(kv, YBIT)
+    kv_low, kv_high = swap(kv_x[:split], YBIT), swap(kv_y[split:], XBIT)
+    kv_mine = [kv, kv_x, kv_y, kv_low, kv_high]
+    kv_all = kv_mine + [swap(piece, CORE) for piece in kv_mine]
+
+    q = pl.pallas_call(
+        functools.partial(q_kernel, planes, scale),
+        out_shape=sds((rows, planes * 2 * LANES), BF),
+        in_specs=[VM, VM] + [ANY] * 10,
+        out_specs=VM,
+        scratch_shapes=[pltpu.VMEM((planes, width, 3 * LANES), BF), dma((planes, 8))],
+        compiler_params=params(),
+        cost_estimate=cost(2 * rows * width * planes * 2 * LANES, w_size),
+        name="q_project",
+    )(x, tables, *qo_w)
+
+    def kv_specs(base):
+        full = pl.BlockSpec((rows, 3 * LANES), lambda i: (0, i + base))
+        part_spec = pl.BlockSpec((split, 3 * LANES), lambda i: (0, i + base))
+        return [full, full, full, part_spec, part_spec] * 2
+
+    seq = rows * group
+    heads = planes * 3
+    att, att_low, lse = pl.pallas_call(
+        attend_kernel,
+        grid=(planes,),
+        out_shape=(
+            sds((rows, planes * 2 * LANES), F32),
+            sds((rows, planes * 2 * LANES), BF),
+            sds((planes, 8, rows), F32),
+        ),
+        in_specs=[
+            pl.BlockSpec((rows, 2 * LANES), lambda i: (0, i)),
+            pl.BlockSpec((8, rows), lambda i: (0, 0)),
+        ]
+        + kv_specs(0),
+        out_specs=(
+            pl.BlockSpec((rows, 2 * LANES), lambda i: (0, i)),
+            pl.BlockSpec((rows, 2 * LANES), lambda i: (0, i)),
+            pl.BlockSpec((1, 8, rows), lambda i: (i, 0, 0)),
+        ),
+        scratch_shapes=[pltpu.VMEM((rows, seq), F32)],
+        compiler_params=params(),
+        cost_estimate=cost(16 * rows * seq * LANES * heads, seq * 3 * LANES * planes * 2),
+        name="attend",
+    )(q, bias, *kv_all)
+
+    ffn_size = planes * group * slab * 3 * ff * 2
+    layer_out, dz2, dffn, flow, scaled, inv, sums_two, gate, up = pl.pallas_call(
+        functools.partial(forward_kernel, planes),
+        out_shape=(
+            sds((rows, width), BF),
+            sds((rows, width), F32),
+            sds((rows, width), BF),
+            sds((rows, width), BF),
+            sds((rows, width), F32),
+            sds((rows, LANES), F32),
+            sds((8, width), F32),
+            sds((planes, rows, ff), F32),
+            sds((planes, rows, ff), F32),
+        ),
+        in_specs=[VM] * 4 + [ANY] * 20,
+        out_specs=(VM,) * 7 + (ANY, ANY),
+        scratch_shapes=[
+            pltpu.VMEM((planes, width, 3 * LANES), BF),
+            pltpu.VMEM((planes, width, 3 * ff), BF),
+            pltpu.VMEM((planes, 2, rows, ff), F32),
+            dma((planes, 8)),
+            dma((planes, 8)),
+            dma((planes, 2)),
+        ],
+        compiler_params=params(),
+        cost_estimate=cost(6 * rows * width * planes * ff, ffn_size),
+        name="forward",
+    )(x, cot, att_low, norms, *qo_w, *ffn_w)
+
+    dfirst = dz2
+    ffn_sums = {}
+    for p in reversed(range(planes)):
+        order = X_FIRST if p % 2 else Y_FIRST
+        gate_spec = pl.BlockSpec((1, rows, ff), functools.partial(lambda p, i: (p, 0, 0), p))
+        whole = pl.BlockSpec((rows, width), lambda i: (0, 0))
+        dfirst, keep, send = pl.pallas_call(
+            functools.partial(ffn_back_kernel, p, order, slab),
+            grid=(1,),
+            out_shape=(
+                sds((rows, width), F32),
+                sds((4, slab, 3 * ff), BF),
+                sds((4, slab, 3 * ff), BF),
+            ),
+            in_specs=[whole, whole, whole, gate_spec, gate_spec] + [ANY] * 10,
+            out_specs=(whole, ANY, ANY),
+            scratch_shapes=[
+                pltpu.VMEM((width, 3 * ff), BF),
+                pltpu.VMEM((3, width, ff), BF),
+                dma((8,)),
+                dma((3, 8)),
+            ],
+            compiler_params=params(),
+            cost_estimate=cost(12 * rows * width * ff, 2 * ffn_size // planes),
+            name="ffn_back",
+        )(dfirst, flow, dffn, gate, up, *ffn_w)
+        first, second = (XBIT, YBIT) if p % 2 else (YBIT, XBIT)
+        ffn_sums[p] = scatter_plane(keep, send, first, second)
+        if p:
+            ffn_sums[p] = swap(ffn_sums[p].astype(BF), 0, p).astype(F32)
+    ffn_grad = sum(ffn_sums[p] for p in range(planes))
+
+    pair = planes // 2
+    grad_shape = lambda columns: sds((4, pair, slab, columns), BF)
+    dz1, dat, delta, sums_one, keep_x, send_x, keep_y, send_y = pl.pallas_call(
+        functools.partial(branch_back_kernel, planes, slab),
+        out_shape=(
+            sds((rows, width), F32),
+            sds((rows, planes * 2 * LANES), BF),
+            sds((planes, 8, rows), F32),
+            sds((8, width), F32),
+        )
+        + (grad_shape(2 * LANES),) * 4,
+        in_specs=[VM] * 6 + [ANY] * 10,
+        out_specs=(VM,) * 4 + (ANY,) * 4,
+        scratch_shapes=[
+            pltpu.VMEM((planes, width, 3 * LANES), BF),
+            pltpu.VMEM((planes, width, 2 * LANES), BF),
+            dma((planes, 8)),
+            dma((planes, 8)),
+        ],
+        compiler_params=params(),
+        cost_estimate=cost(4 * rows * width * planes * 2 * LANES, 2 * w_size),
+        name="branch_back",
+    )(dfirst, scaled, inv, norms, att, att_low, *qo_w)
+
+    def scatter_all(keep_x, send_x, keep_y, send_y):
+        sum_x = scatter_plane(keep_x, send_x, XBIT, YBIT)
+        sum_y = scatter_plane(keep_y, send_y, YBIT, XBIT)
+        blocks = [sum_x[k] for k in range(pair)] + [sum_y[k] for k in range(pair)]
+        total = blocks[0]
+        for j in range(1, planes):
+            total = total + swap(blocks[j].astype(BF), 0, j).astype(F32)
+        return total
+
+    o_grad = scatter_all(keep_x, send_x, keep_y, send_y)
+
+    sums = jnp.concatenate([sums_one[0:1], sums_two[0:1], sums_one[1:2], sums_two[1:2]], axis=0)
+    sums = jnp.concatenate([sums, jnp.zeros((4, width), F32)], axis=0)
+    for mask in (CORE, XBIT, YBIT):
+        sums = sums + swap(sums, mask)
+    for mask in range(planes.bit_length() - 1):
+        sums = sums + swap(sums, 0, 1 << mask)
+    sums = lax.dynamic_slice_in_dim(sums, dp * slab, slab, 1)
+
+    dq_parts, dkv_parts = [], []
+    for call in range(2):
+        first, second = ((XBIT, YBIT), (YBIT, XBIT))[call]
+        order = order_of(first, second)
+        base = call * pair
+        at = functools.partial(lambda base, i: (0, i + base), base)
+        stat = pl.BlockSpec((1, 8, rows), functools.partial(lambda base, i: (i + base, 0, 0), base))
+        keep, send, dq = pl.pallas_call(
+            functools.partial(attend_back_kernel, order, scale),
+            grid=(pair,),
+            out_shape=(
+                sds((4, rows, pair * 3 * LANES), BF),
+                sds((4, rows, pair * 3 * LANES), BF),
+                sds((rows, pair * 2 * LANES), BF),
+            ),
+            in_specs=[
+                pl.BlockSpec((rows, 2 * LANES), at),
+                pl.BlockSpec((rows, 2 * LANES), at),
+                stat,
+                stat,
+                pl.BlockSpec((rows, 8), lambda i: (0, 0)),
+                pl.BlockSpec((4, rows, LANES), lambda i: (0, 0, 0)),
+            ]
+            + kv_specs(base),
+            out_specs=(
+                pl.BlockSpec((4, rows, 3 * LANES), lambda i: (0, 0, i)),
+                pl.BlockSpec((4, rows, 3 * LANES), lambda i: (0, 0, i)),
+                pl.BlockSpec((rows, 2 * LANES), lambda i: (0, i)),
+            ),
+            compiler_params=params(),
+            cost_estimate=cost(
+                40 * rows * seq * LANES * heads // 2, seq * 3 * LANES * planes * 2
+            ),
+            name="attend_back",
+        )(q, dat, lse, delta, bias_t, tables, *kv_all)
+        dkv_parts.append(scatter_plane(keep, send, first, second))
+        dq_parts.append(dq)
+    dq = jnp.concatenate(dq_parts, axis=1)
+    dkv = jnp.concatenate(dkv_parts, axis=1)
+
+    def project_back(d, acc, pieces, used, mode, out_type):
+        columns = 3 * LANES
+        return pl.pallas_call(
+            functools.partial(project_back_kernel, planes, columns, used, slab, mode),
+            out_shape=(sds((rows, width), out_type),) + (grad_shape(used),) * 4,
+            in_specs=[VM] * 4 + [ANY] * 10,
+            out_specs=(VM,) + (ANY,) * 4,
+            scratch_shapes=[
+                pltpu.VMEM((planes, width, columns), BF),
+                pltpu.VMEM((planes, width, used), BF),
+                dma((planes, 8)),
+                dma((planes, 8)),
+            ],
+            compiler_params=params(),
+            cost_estimate=cost(4 * rows * width * planes * used, 2 * w_size),
+            name="project_back",
+        )(x, d, acc, tables, *pieces)
+
+    din, *q_parts = project_back(dq, dz1, qo_w, 2 * LANES, False, F32)
+    q_grad = scatter_all(*q_parts)
+    din, *kv_parts = project_back(dkv, din, kv_w, 3 * LANES, True, BF)
+    input_grad = exchange_out([din[j * part : (j + 1) * part] for j in range(planes)])
+    kv_grad = scatter_all(*kv_parts)
+
+    layer_rows = exchange_out([layer_out[j * part : (j + 1) * part] for j in range(planes)])
+    shape = hidden_in.shape
+    qkv_grad = jnp.stack(
+        [
+            q_grad[:, : 3 * HEAD_DIM],
+            kv_grad[:, : 3 * HEAD_DIM],
+            jnp.concatenate([kv_grad[:, 2 * LANES :], kv_grad[:, 3 * HEAD_DIM : 2 * LANES]], axis=1),
+        ]
+    )
+    out_grad = jnp.concatenate([o_grad[:, LANES:], o_grad[:, HEAD_DIM:LANES]], axis=1).T
+    return (
+        layer_rows.reshape(shape),
+        input_grad.reshape(shape).astype(F32),
+        qkv_grad,
+        out_grad,
+        jnp.stack([ffn_grad[:, :ff], ffn_grad[:, ff : 2 * ff]]),
+        ffn_grad[:, 2 * ff :].T,
+        sums[0:2],
+        sums[2:4],
+    )
 
 
 def rope_tables(positions, half_dim):
@@ -341,8 +1181,10 @@
 
 
 def solution(mesh):
+    rows_of = dict(mesh.shape)
+    by_plane = rows_of == {"dp": 8, "mp": 4}
     return jax.shard_map(
-        body,
+        plane_body if by_plane else body,
         mesh=mesh,
         in_specs=(
             P(None, ("dp", "mp"), None, None),

time: 1280 us -> 560 us (0.44)
  waiting for transfers between devices: 679 us -> 219 us
  blocking collectives: 278 us -> 0 us
  matrix products: 154 us -> 0 us
  Pallas kernels: 0 us -> 137 us
  starting transfers between devices: 1.83 us -> 124 us
  local copies, waits for them, and re-layouts: 64.9 us -> 22.8 us
  other arithmetic: 74.6 us -> 37.1 us
    reduce_scatter x13 -> x0, waiting for transfers between devices: 317 us -> none  [the longest x4 105 us: body(): lax.psum_scatter(value_total, 'dp', scatter_dimension=2, tiled=True)]
    all_gather x20 -> x0, blocking collectives: 278 us -> none  [the longest x4 73.1 us: body(): lax.all_gather(cotangent[micro_step], 'mp', axis=0, tiled=True)]
    ppermute x0 -> x113, waiting for transfers between devices: none -> 219 us  [swap(): lax.ppermute(value, ('dp', 'mp'), [(i, i ^ mask) for i in range(count)])]
    unnamed x29 -> x0, waiting for transfers between devices: 212 us -> none
    dot_general x68 -> x0, matrix products: 152 us -> none  [the longest x4 19.2 us: score_grads(): jnp.einsum('shqd,shkd->shqk', grad_part, value_part, preferred_element_ty...]
    psum x4 -> x0, waiting for transfers between devices: 150 us -> none  [the longest x2 86.1 us: body(): lax.psum(jnp.einsum('rscf,cdf->rsd', d_gate_up, gate_up_matrix, preferred...]
    pallas_call x0 -> x13, Pallas kernels: none -> 137 us  [the longest x4 44.6 us: plane_body(): pl.pallas_call(functools.partial(ffn_back_kernel, p, order, slab), grid=(...]
    ppermute x0 -> x113, starting transfers between devices: none -> 124 us  [swap(): lax.ppermute(value, ('dp', 'mp'), [(i, i ^ mask) for i in range(count)])]
  transfers between devices with their start and end apart: 24 -> 113, of which waited for: 20 -> 47; matrix products, arithmetic and copies ran while one was open for 15% -> 10% of each run, Pallas kernels for 0% -> 22%
where the time goes in v1:
time: 560 us; the launch traced here: 550 us
  waiting for transfers between devices  219 us (39%)
  Pallas kernels  137 us (24%)
  starting transfers between devices  124 us (22%)
  other arithmetic  37.1 us (7%)
  local copies, waits for them, and re-layouts  22.8 us (4%)
  between operations  10.2 us (2%)
    ppermute x113, waiting for transfers between devices, swap(): lax.ppermute(value, ('dp', 'mp'), [(i, i ^ mask) for i in range(count)])  219 us
    ppermute x113, starting transfers between devices, swap(): lax.ppermute(value, ('dp', 'mp'), [(i, i ^ mask) for i in range(count)])  124 us
    pallas_call x4, Pallas kernels, plane_body(): pl.pallas_call(functools.partial(ffn_back_kernel, p, order, slab), grid=(...  44.6 us
    pallas_call x2, Pallas kernels, plane_body(): pl.pallas_call(functools.partial(attend_back_kernel, order, scale), grid=...  31.2 us
    pallas_call x1, Pallas kernels, plane_body(): pl.pallas_call(functools.partial(forward_kernel, planes), out_shape=(sds(...  15.6 us
    pallas_call x1, Pallas kernels, plane_body(): pl.pallas_call(attend_kernel, grid=(planes,), out_shape=(sds((rows, plane...  14.1 us
    pallas_call x2, Pallas kernels, project_back(): pl.pallas_call(functools.partial(project_back_kernel, planes, columns, us...  13.4 us
    convert_element_type x24, other arithmetic, add_low(): return (a.astype(F32) + b.astype(F32)).astype(BF)  13 us
  transfers between devices with their start and end apart: 113, of which 47 were waited for; matrix products, arithmetic and copies ran while one was open for 10% of the time, Pallas kernels for 22%

profile of v1, /device:TPU:0, one launch (start us, length us, event | category | flops | bytes accessed | tf_op | source)
XLA Modules:
  0.0 550.2 jit_solution(3684475855021389354)
XLA Ops:
  43.8 8.5 %collective-permute-start.43 = (bf16[96,2304]{1,0:T(8,128)(2,1)S(1)}, bf16[96,2304]{1,0:T(8,128)(2,1)S(1)}, u32[]{:S(2)}, u32[]{:S(2)}) collective-permute-start(bf16[96,2304]{1,0:T(8,128)(2,1)S(1)} %get-tuple-element.140), channel_id=1, source_target_pairs={{0,2},{1,3},{2,0},{3,1},{4,6},{5,7},{6,4},{7,5},{8,10},{9,11},{10,... | collective-permute-start | bytes 1327112 | tf_op jit(solution)/shard_map/ppermute | solution.py:29
  62.1 10.6 %collective-permute-start.1 = (bf16[64,768]{1,0:T(8,128)(2,1)S(1)}, bf16[64,768]{1,0:T(8,128)(2,1)S(1)}, u32[]{:S(2)}, u32[]{:S(2)}) collective-permute-start(bf16[64,768]{1,0:T(8,128)(2,1)S(1)} %get-tuple-element.164), channel_id=1, source_target_pairs={{0,2},{1,3},{2,0},{3,1},{4,6},{5,7},{6,4},{7,5},{8,10},{9,11},{10,... | collective-permute-start | bytes 294920 | tf_op jit(solution)/shard_map/ppermute | solution.py:29
  72.8 17.6 %collective-permute-done.1 = bf16[64,768]{1,0:T(8,128)(2,1)S(1)} collective-permute-done((bf16[64,768]{1,0:T(8,128)(2,1)S(1)}, bf16[64,768]{1,0:T(8,128)(2,1)S(1)}, u32[]{:S(2)}, u32[]{:S(2)}) %collective-permute-start.1) | collective-permute-done | bytes 98336 | tf_op jit(solution)/shard_map/ppermute | solution.py:29
  108.6 5.5 %kv_project.1.refs_0_ = bf16[256,1536]{1,0:T(8,128)(2,1)} custom-call(bf16[256,768]{1,0:T(8,128)(2,1)} %pad_maximum_fusion.6.x_ref, f32[4,256,128]{2,1,0:T(8,128)} %pad_maximum_fusion.3.tab_ref, bf16[4,96,384]{2,1,0:T(8,128)(2,1)} %copy-done.7, bf16[4,96,384]{2,1,0:T(8,128)(2,1)} %copy-done.12, bf16[4,96,384]{2,1,0:T(8,128)(2,1)} %copy-done.11, ...), custom_call_target="tpu_custom_call" | custom-call | flops 603979776 | bytes 2359296 | tf_op jit(solution)/shard_map/kv_project/pallas_call | solution.py:605
  117.1 28.1 %collective-permute-done.11.refs_3_ = bf16[2,96,384]{2,1,0:T(8,128)(2,1)} collective-permute-done((bf16[2,96,384]{2,1,0:T(8,128)(2,1)}, bf16[2,96,384]{2,1,0:T(8,128)(2,1)}, u32[]{:S(2)}, u32[]{:S(2)}) %collective-permute-start.11) | collective-permute-done | bytes 147488 | tf_op jit(solution)/shard_map/ppermute | solution.py:29
  149.2 11.2 %collective-permute-done.31.refs_2_ = bf16[256,1536]{1,0:T(8,128)(2,1)} collective-permute-done((bf16[256,1536]{1,0:T(8,128)(2,1)}, bf16[256,1536]{1,0:T(8,128)(2,1)}, u32[]{:S(2)}, u32[]{:S(2)}) %collective-permute-start.31) | collective-permute-done | bytes 786464 | tf_op jit(solution)/shard_map/ppermute | solution.py:29
  169.6 7.5 %collective-permute-done.33.refs_4_ = bf16[128,1536]{1,0:T(8,128)(2,1)S(1)} collective-permute-done((bf16[128,1536]{1,0:T(8,128)(2,1)S(1)}, bf16[128,1536]{1,0:T(8,128)(2,1)S(1)}, u32[]{:S(2)}, u32[]{:S(2)}) %collective-permute-start.33) | collective-permute-done | bytes 393248 | tf_op jit(solution)/shard_map/ppermute | solution.py:29
  198.5 7.9 %collective-permute-done.48.refs_14_.refs_4_ = bf16[2,96,2304]{2,1,0:T(8,128)(2,1)} collective-permute-done((bf16[2,96,2304]{2,1,0:T(8,128)(2,1)}, bf16[2,96,2304]{2,1,0:T(8,128)(2,1)}, u32[]{:S(2)}, u32[]{:S(2)}) %collective-permute-start.48) | collective-permute-done | bytes 884768 | tf_op jit(solution)/shard_map/ppermute | solution.py:29
  207.5 14.1 %attend.1 = (f32[256,1024]{1,0:T(8,128)}, bf16[256,1024]{1,0:T(8,128)(2,1)}, f32[4,8,256]{2,1,0:T(8,128)}) custom-call(bf16[256,1024]{1,0:T(8,128)(2,1)} %q_project.1.q_ref, f32[8,256]{1,0:T(8,128)} %fusion.39.bias_ref, bf16[256,1536]{1,0:T(8,128)(2,1)} %kv_project.1.refs_0_, bf16[256,1536]{1,0:T(8,128)(2,1)} %collective-permute-done.30.refs_1_, ...), custom_call_target="tpu_custom_call" | custom-call | flops 12884901888 | bytes 6291456 | tf_op jit(solution)/shard_map/attend/pallas_call | solution.py:640
  221.6 15.6 %forward.1 = (bf16[256,768]{1,0:T(8,128)(2,1)}, f32[256,768]{1,0:T(8,128)}, bf16[256,768]{1,0:T(8,128)(2,1)}, bf16[256,768]{1,0:T(8,128)(2,1)}, f32[256,768]{1,0...) custom-call(bf16[256,768]{1,0:T(8,128)(2,1)} %pad_maximum_fusion.6.x_ref, ...), custom_call_target="tpu_custom_call" | custom-call | flops 3623878656 | bytes 14155776 | tf_op jit(solution)/shard_map/forward/pallas_call | solution.py:665
  243.5 8.1 %ffn_back.4 = (f32[256,768]{1,0:T(8,128)}, bf16[4,96,2304]{2,1,0:T(8,128)(2,1)}, bf16[4,96,2304]{2,1,0:T(8,128)(2,1)}) custom-call(f32[256,768]{1,0:T(8,128)} %get-tuple-element.58.acc_ref, bf16[256,768]{1,0:T(8,128)(2,1)} %get-tuple-element.59.flow_ref, bf16[256,768]{1,0:T(8,128)(2,1)} %get-tuple-element.60.dffn_ref, ...), custom_call_target="tpu_custom_call" | custom-call | flops 1811939328 | bytes 7077888 | tf_op jit(solution)/shard_map/ffn_back/pallas_call | solution.py:699
  251.6 8.1 %ffn_back.5 = (f32[256,768]{1,0:T(8,128)}, bf16[4,96,2304]{2,1,0:T(8,128)(2,1)}, bf16[4,96,2304]{2,1,0:T(8,128)(2,1)}) custom-call(f32[256,768]{1,0:T(8,128)} %get-tuple-element.63.acc_ref, bf16[256,768]{1,0:T(8,128)(2,1)} %get-tuple-element.59.flow_ref, bf16[256,768]{1,0:T(8,128)(2,1)} %get-tuple-element.60.dffn_ref, ...), custom_call_target="tpu_custom_call" | custom-call | flops 1811939328 | bytes 7077888 | tf_op jit(solution)/shard_map/ffn_back/pallas_call | solution.py:699
  259.7 20.5 %ffn_back.6 = (f32[256,768]{1,0:T(8,128)}, bf16[4,96,2304]{2,1,0:T(8,128)(2,1)}, bf16[4,96,2304]{2,1,0:T(8,128)(2,1)}) custom-call(f32[256,768]{1,0:T(8,128)} %get-tuple-element.64.acc_ref, bf16[256,768]{1,0:T(8,128)(2,1)} %get-tuple-element.59.flow_ref, bf16[256,768]{1,0:T(8,128)(2,1)} %get-tuple-element.60.dffn_ref, ...), custom_call_target="tpu_custom_call" | custom-call | flops 1811939328 | bytes 7077888 | tf_op jit(solution)/shard_map/ffn_back/pallas_call | solution.py:699
  280.2 8.0 %ffn_back.7 = (f32[256,768]{1,0:T(8,128)}, bf16[4,96,2304]{2,1,0:T(8,128)(2,1)}, bf16[4,96,2304]{2,1,0:T(8,128)(2,1)}) custom-call(f32[256,768]{1,0:T(8,128)} %get-tuple-element.65.acc_ref, bf16[256,768]{1,0:T(8,128)(2,1)} %get-tuple-element.59.flow_ref, bf16[256,768]{1,0:T(8,128)(2,1)} %get-tuple-element.60.dffn_ref, ...), custom_call_target="tpu_custom_call" | custom-call | flops 1811939328 | bytes 7077888 | tf_op jit(solution)/shard_map/ffn_back/pallas_call | solution.py:699
  288.2 7.0 %branch_back.1 = (f32[256,768]{1,0:T(8,128)}, bf16[256,1024]{1,0:T(8,128)(2,1)}, f32[4,8,256]{2,1,0:T(8,128)}, f32[8,768]{1,0:T(8,128)}, bf16[4,2,96,256]{3,2,1,...) custom-call(f32[256,768]{1,0:T(8,128)} %get-tuple-element.66.dfirst_, ...), custom_call_target="tpu_custom_call" | custom-call | flops 805306368 | bytes 4718592 | tf_op jit(solution)/shard_map/branch_back/pallas_call | solution.py:727
  296.6 15.6 %attend_back.3 = (bf16[4,256,768]{2,1,0:T(8,128)(2,1)}, bf16[4,256,768]{2,1,0:T(8,128)(2,1)}, bf16[256,512]{1,0:T(8,128)(2,1)}) custom-call(bf16[256,1024]{1,0:T(8,128)(2,1)} %q_project.1.q_ref, bf16[256,1024]{1,0:T(8,128)(2,1)} %get-tuple-element.70.dat_ref, f32[4,8,256]{2,1,0:T(8,128)} %get-tuple-element.71.lse_ref, ...), custom_call_target="tpu_custom_call" | custom-call | flops 16106127360 | bytes 6291456 | tf_op jit(solution)/shard_map/attend_back/pallas_call | solution.py:775
  312.3 15.5 %attend_back.2 = (bf16[4,256,768]{2,1,0:T(8,128)(2,1)}, bf16[4,256,768]{2,1,0:T(8,128)(2,1)}, bf16[256,512]{1,0:T(8,128)(2,1)}) custom-call(bf16[256,1024]{1,0:T(8,128)(2,1)} %q_project.1.q_ref, bf16[256,1024]{1,0:T(8,128)(2,1)} %get-tuple-element.70.dat_ref, f32[4,8,256]{2,1,0:T(8,128)} %get-tuple-element.71.lse_ref, ...), custom_call_target="tpu_custom_call" | custom-call | flops 16106127360 | bytes 6291456 | tf_op jit(solution)/shard_map/attend_back/pallas_call | solution.py:775
  332.3 6.1 %project_back.2 = (f32[256,768]{1,0:T(8,128)}, bf16[4,2,96,256]{3,2,1,0:T(8,128)(2,1)}, bf16[4,2,96,256]{3,2,1,0:T(8,128)(2,1)}, bf16[4,2,96,256]{3,2,1,0:T(8,128)(2,1)}, bf16[4,2,96,256]{3,2,1,0:T(8,128)(2,1)}) custom-call(bf16[256,768]{1,0:T(8,128)(2,1)} %pad_maximum_fusion.6.x_ref, bf16[256,1024]{1,0:T(8,128)(2,1)} %pad_maximum_fusion.4.d_ref, ...), custom_call_target="tpu_custom_call" | custom-call | flops 805306368 | bytes 4718592 | tf_op jit(solution)/shard_map/project_back/pallas_call | solution.py:810
  411.9 7.4 %collective-permute-done.61 = bf16[2,256,768]{2,1,0:T(8,128)(2,1)S(1)} collective-permute-done((bf16[2,256,768]{2,1,0:T(8,128)(2,1)S(1)}, bf16[2,256,768]{2,1,0:T(8,128)(2,1)S(1)}, u32[]{:S(2)}, u32[]{:S(2)}) %collective-permute-start.61) | collective-permute-done | bytes 786464 | tf_op jit(solution)/shard_map/ppermute | solution.py:29
  424.9 16.8 %collective-permute-done.105 = bf16[2,96,2304]{2,1,0:T(8,128)(2,1)S(1)} collective-permute-done((bf16[2,96,2304]{2,1,0:T(8,128)(2,1)S(1)}, bf16[2,96,2304]{2,1,0:T(8,128)(2,1)S(1)}, u32[]{:S(2)}, u32[]{:S(2)}) %collective-permute-start.105) | collective-permute-done | bytes 884768 | tf_op jit(solution)/shard_map/ppermute | solution.py:29
  445.6 11.6 %collective-permute-done.94 = bf16[2,96,2304]{2,1,0:T(8,128)(2,1)S(1)} collective-permute-done((bf16[2,96,2304]{2,1,0:T(8,128)(2,1)S(1)}, bf16[2,96,2304]{2,1,0:T(8,128)(2,1)S(1)}, u32[]{:S(2)}, u32[]{:S(2)}) %collective-permute-start.94) | collective-permute-done | bytes 884768 | tf_op jit(solution)/shard_map/ppermute | solution.py:29
  459.6 9.5 %collective-permute-done.62 = bf16[256,768]{1,0:T(8,128)(2,1)S(1)} collective-permute-done((bf16[256,768]{1,0:T(8,128)(2,1)S(1)}, bf16[256,768]{1,0:T(8,128)(2,1)S(1)}, u32[]{:S(2)}, u32[]{:S(2)}) %collective-permute-start.62) | collective-permute-done | bytes 393248 | tf_op jit(solution)/shard_map/ppermute | solution.py:29
  470.8 7.3 %project_back.3 = (bf16[256,768]{1,0:T(8,128)(2,1)}, bf16[4,2,96,384]{3,2,1,0:T(8,128)(2,1)}, bf16[4,2,96,384]{3,2,1,0:T(8,128)(2,1)}, bf16[4,2,96,384]{3,2,1,0:T(8,128)(2,1)}, bf16[4,2,96,384]{3,2,1,0:T(8,128)(2,1)}) custom-call(bf16[256,768]{1,0:T(8,128)(2,1)} %pad_maximum_fusion.6.x_ref, f32[256,1536]{1,0:T(8,128)} %pad_maximum_fusion.1.d_ref, ...), custom_call_target="tpu_custom_call" | custom-call | flops 1207959552 | bytes 4718592 | tf_op jit(solution)/shard_map/project_back/pallas_call | solution.py:810
  508.1 25.0 %collective-permute-done.103 = bf16[96,2304]{1,0:T(8,128)(2,1)S(1)} collective-permute-done((bf16[96,2304]{1,0:T(8,128)(2,1)S(1)}, bf16[96,2304]{1,0:T(8,128)(2,1)S(1)}, u32[]{:S(2)}, u32[]{:S(2)}) %collective-permute-start.103) | collective-permute-done | bytes 442400 | tf_op jit(solution)/shard_map/ppermute | solution.py:29
  (474 shorter events, 247.0 us)
Async XLA Ops:
  43.8 49.6 %collective-permute-start.43 = (bf16[96,2304]{1,0:T(8,128)(2,1)S(1)}, bf16[96,2304]{1,0:T(8,128)(2,1)S(1)}, u32[]{:S(2)}, u32[]{:S(2)}) collective-permute-start(bf16[96,2304]{1,0:T(8,128)(2,1)S(1)} %get-tuple-element.140), channel_id=1, source_target_pairs={{0,2},{1,3},{2,0},{3,1},{4,6},{5,7},{6,4},{7,5},{8,10},{9,11},{10,... | collective-permute-start | bytes 1327112 | tf_op jit(solution)/shard_map/ppermute | solution.py:29
  52.4 41.5 %collective-permute-start.42 = (bf16[96,2304]{1,0:T(8,128)(2,1)S(1)}, bf16[96,2304]{1,0:T(8,128)(2,1)S(1)}, u32[]{:S(2)}, u32[]{:S(2)}) collective-permute-start(bf16[96,2304]{1,0:T(8,128)(2,1)S(1)} %get-tuple-element.140), channel_id=1, source_target_pairs={{0,1},{1,0},{2,3},{3,2},{4,5},{5,4},{6,7},{7,6},{8,9},{9,8},{10,11... | collective-permute-start | bytes 1327112 | tf_op jit(solution)/shard_map/ppermute | solution.py:29
  52.5 42.0 %collective-permute-start.44 = (bf16[96,2304]{1,0:T(8,128)(2,1)S(1)}, bf16[96,2304]{1,0:T(8,128)(2,1)S(1)}, u32[]{:S(2)}, u32[]{:S(2)}) collective-permute-start(bf16[96,2304]{1,0:T(8,128)(2,1)S(1)} %get-tuple-element.140), channel_id=1, source_target_pairs={{0,3},{1,2},{2,1},{3,0},{4,7},{5,6},{6,5},{7,4},{8,11},{9,10},{10,... | collective-permute-start | bytes 1327112 | tf_op jit(solution)/shard_map/ppermute | solution.py:29
  100.5 78.9 %collective-permute-start.46 = (bf16[4,96,2304]{2,1,0:T(8,128)(2,1)S(1)}, bf16[4,96,2304]{2,1,0:T(8,128)(2,1)S(1)}, u32[]{:S(2)}, u32[]{:S(2)}) collective-permute-start(bf16[4,96,2304]{2,1,0:T(8,128)(2,1)S(1)} %pad_maximum_fusion.refs_10_.refs_0_), channel_id=1, source_target_pairs={{0,16},{1,17},{2,18},{3,19},{4,20},{5,21},{6,22},{7,23},{8,24},{9,... | collective-permute-start | bytes 5308424 | tf_op jit(solution)/shard_map/ppermute | solution.py:29
  106.6 38.7 %collective-permute-start.11 = (bf16[2,96,384]{2,1,0:T(8,128)(2,1)}, bf16[2,96,384]{2,1,0:T(8,128)(2,1)}, u32[]{:S(2)}, u32[]{:S(2)}) collective-permute-start(bf16[2,96,384]{2,1,0:T(8,128)(2,1)} %slice.637), channel_id=1, source_target_pairs={{0,16},{1,17},{2,18},{3,19},{4,20},{5,21},{6,22},{7,23},{8,24},{9,... | collective-permute-start | bytes 442376 | tf_op jit(solution)/shard_map/ppermute | solution.py:29
  107.2 72.7 %collective-permute-start.45 = (bf16[4,96,2304]{2,1,0:T(8,128)(2,1)S(1)}, bf16[4,96,2304]{2,1,0:T(8,128)(2,1)}, u32[]{:S(2)}, u32[]{:S(2)}) collective-permute-start(bf16[4,96,2304]{2,1,0:T(8,128)(2,1)S(1)} %pad_maximum_fusion.refs_10_.refs_0_), channel_id=1, source_target_pairs={{0,8},{1,9},{2,10},{3,11},{4,12},{5,13},{6,14},{7,15},{8,0},{9,1},... | collective-permute-start | bytes 5308424 | tf_op jit(solution)/shard_map/ppermute | solution.py:29
  114.2 46.2 %collective-permute-start.31 = (bf16[256,1536]{1,0:T(8,128)(2,1)}, bf16[256,1536]{1,0:T(8,128)(2,1)}, u32[]{:S(2)}, u32[]{:S(2)}) collective-permute-start(bf16[256,1536]{1,0:T(8,128)(2,1)} %kv_project.1.refs_0_), channel_id=1, source_target_pairs={{0,16},{1,17},{2,18},{3,19},{4,20},{5,21},{6,22},{7,23},{8,24},{9,... | collective-permute-start | bytes 2359304 | tf_op jit(solution)/shard_map/ppermute | solution.py:29
  115.7 50.7 %collective-permute-start.30 = (bf16[256,1536]{1,0:T(8,128)(2,1)}, bf16[256,1536]{1,0:T(8,128)(2,1)}, u32[]{:S(2)}, u32[]{:S(2)}) collective-permute-start(bf16[256,1536]{1,0:T(8,128)(2,1)} %kv_project.1.refs_0_), channel_id=1, source_target_pairs={{0,8},{1,9},{2,10},{3,11},{4,12},{5,13},{6,14},{7,15},{8,0},{9,1},... | collective-permute-start | bytes 2359304 | tf_op jit(solution)/shard_map/ppermute | solution.py:29
  186.6 35.0 %collective-permute-start.49 = (bf16[4,96,2304]{2,1,0:T(8,128)(2,1)S(1)}, bf16[4,96,2304]{2,1,0:T(8,128)(2,1)}, u32[]{:S(2)}, u32[]{:S(2)}) collective-permute-start(bf16[4,96,2304]{2,1,0:T(8,128)(2,1)S(1)} %pad_maximum_fusion.refs_10_.refs_0_), channel_id=1, source_target_pairs={{0,4},{1,5},{2,6},{3,7},{4,0},{5,1},{6,2},{7,3},{8,12},{9,13},{10,... | collective-permute-start | bytes 5308424 | tf_op jit(solution)/shard_map/ppermute | solution.py:29
  186.7 34.9 %collective-permute-start.51 = (bf16[4,96,2304]{2,1,0:T(8,128)(2,1)S(1)}, bf16[4,96,2304]{2,1,0:T(8,128)(2,1)}, u32[]{:S(2)}, u32[]{:S(2)}) collective-permute-start(bf16[4,96,2304]{2,1,0:T(8,128)(2,1)S(1)} %collective-permute-done.46.refs_12_.refs_2_), channel_id=1, source_target_pairs={{0,4},{1,5},{2,6},{3,7},{4,0},{5,1},{6,2},{7,3},{8,12},{9,13},{10,... | collective-permute-start | bytes 5308424 | tf_op jit(solution)/shard_map/ppermute | solution.py:29
  239.1 99.4 %collective-permute-start.56 = (bf16[64,768]{1,0:T(8,128)(2,1)S(1)}, bf16[64,768]{1,0:T(8,128)(2,1)S(1)}, u32[]{:S(2)}, u32[]{:S(2)}) collective-permute-start(bf16[64,768]{1,0:T(8,128)(2,1)S(1)} %get-tuple-element.154), channel_id=1, source_target_pairs={{0,3},{1,2},{2,1},{3,0},{4,7},{5,6},{6,5},{7,4},{8,11},{9,10},{10,... | collective-permute-start | bytes 294920 | tf_op jit(solution)/shard_map/ppermute | solution.py:29
  241.4 97.7 %collective-permute-start.55 = (bf16[64,768]{1,0:T(8,128)(2,1)S(1)}, bf16[64,768]{1,0:T(8,128)(2,1)S(1)}, u32[]{:S(2)}, u32[]{:S(2)}) collective-permute-start(bf16[64,768]{1,0:T(8,128)(2,1)S(1)} %get-tuple-element.155), channel_id=1, source_target_pairs={{0,2},{1,3},{2,0},{3,1},{4,6},{5,7},{6,4},{7,5},{8,10},{9,11},{10,... | collective-permute-start | bytes 294920 | tf_op jit(solution)/shard_map/ppermute | solution.py:29
  241.4 97.8 %collective-permute-start.54 = (bf16[64,768]{1,0:T(8,128)(2,1)S(1)}, bf16[64,768]{1,0:T(8,128)(2,1)S(1)}, u32[]{:S(2)}, u32[]{:S(2)}) collective-permute-start(bf16[64,768]{1,0:T(8,128)(2,1)S(1)} %get-tuple-element.156), channel_id=1, source_target_pairs={{0,1},{1,0},{2,3},{3,2},{4,5},{5,4},{6,7},{7,6},{8,9},{9,8},{10,11... | collective-permute-start | bytes 294920 | tf_op jit(solution)/shard_map/ppermute | solution.py:29
  251.5 150.7 %collective-permute-start.104 = (bf16[4,96,2304]{2,1,0:T(8,128)(2,1)}, bf16[4,96,2304]{2,1,0:T(8,128)(2,1)S(1)}, u32[]{:S(2)}, u32[]{:S(2)}) collective-permute-start(bf16[4,96,2304]{2,1,0:T(8,128)(2,1)} %get-tuple-element.101), channel_id=1, source_target_pairs={{0,4},{1,5},{2,6},{3,7},{4,0},{5,1},{6,2},{7,3},{8,12},{9,13},{10,... | collective-permute-start | bytes 5308424 | tf_op jit(solution)/shard_map/ppermute | solution.py:29
  348.4 48.0 %collective-permute-start.60 = (bf16[4,256,768]{2,1,0:T(8,128)(2,1)}, bf16[4,256,768]{2,1,0:T(8,128)(2,1)}, u32[]{:S(2)}, u32[]{:S(2)}) collective-permute-start(bf16[4,256,768]{2,1,0:T(8,128)(2,1)} %get-tuple-element.76), channel_id=1, source_target_pairs={{0,4},{1,5},{2,6},{3,7},{4,0},{5,1},{6,2},{7,3},{8,12},{9,13},{10,... | collective-permute-start | bytes 4718600 | tf_op jit(solution)/shard_map/ppermute | solution.py:29
  349.0 49.8 %collective-permute-start.57 = (bf16[4,256,768]{2,1,0:T(8,128)(2,1)}, bf16[4,256,768]{2,1,0:T(8,128)(2,1)}, u32[]{:S(2)}, u32[]{:S(2)}) collective-permute-start(bf16[4,256,768]{2,1,0:T(8,128)(2,1)} %get-tuple-element.74), channel_id=1, source_target_pairs={{0,4},{1,5},{2,6},{3,7},{4,0},{5,1},{6,2},{7,3},{8,12},{9,13},{10,... | collective-permute-start | bytes 4718600 | tf_op jit(solution)/shard_map/ppermute | solution.py:29
  404.9 36.9 %collective-permute-start.105 = (bf16[2,96,2304]{2,1,0:T(8,128)(2,1)S(1)}, bf16[2,96,2304]{2,1,0:T(8,128)(2,1)S(1)}, u32[]{:S(2)}, u32[]{:S(2)}) collective-permute-start(bf16[2,96,2304]{2,1,0:T(8,128)(2,1)S(1)} %get-tuple-element.119), channel_id=1, source_target_pairs={{0,8},{1,9},{2,10},{3,11},{4,12},{5,13},{6,14},{7,15},{8,0},{9,1},... | collective-permute-start | bytes 2654216 | tf_op jit(solution)/shard_map/ppermute | solution.py:29
  407.9 35.3 %collective-permute-start.101 = (bf16[2,96,2304]{2,1,0:T(8,128)(2,1)S(1)}, bf16[2,96,2304]{2,1,0:T(8,128)(2,1)S(1)}, u32[]{:S(2)}, u32[]{:S(2)}) collective-permute-start(bf16[2,96,2304]{2,1,0:T(8,128)(2,1)S(1)} %get-tuple-element.117), channel_id=1, source_target_pairs={{0,16},{1,17},{2,18},{3,19},{4,20},{5,21},{6,22},{7,23},{8,24},{9,... | collective-permute-start | bytes 2654216 | tf_op jit(solution)/shard_map/ppermute | solution.py:29
  408.4 48.8 %collective-permute-start.94 = (bf16[2,96,2304]{2,1,0:T(8,128)(2,1)S(1)}, bf16[2,96,2304]{2,1,0:T(8,128)(2,1)S(1)}, u32[]{:S(2)}, u32[]{:S(2)}) collective-permute-start(bf16[2,96,2304]{2,1,0:T(8,128)(2,1)S(1)} %get-tuple-element.113), channel_id=1, source_target_pairs={{0,16},{1,17},{2,18},{3,19},{4,20},{5,21},{6,22},{7,23},{8,24},{9,... | collective-permute-start | bytes 2654216 | tf_op jit(solution)/shard_map/ppermute | solution.py:29
  419.3 62.5 %collective-permute-start.97 = (bf16[2,96,2304]{2,1,0:T(8,128)(2,1)}, bf16[2,96,2304]{2,1,0:T(8,128)(2,1)}, u32[]{:S(2)}, u32[]{:S(2)}) collective-permute-start(bf16[2,96,2304]{2,1,0:T(8,128)(2,1)} %get-tuple-element.115), channel_id=1, source_target_pairs={{0,8},{1,9},{2,10},{3,11},{4,12},{5,13},{6,14},{7,15},{8,0},{9,1},... | collective-permute-start | bytes 2654216 | tf_op jit(solution)/shard_map/ppermute | solution.py:29
  422.8 46.3 %collective-permute-start.62 = (bf16[256,768]{1,0:T(8,128)(2,1)S(1)}, bf16[256,768]{1,0:T(8,128)(2,1)S(1)}, u32[]{:S(2)}, u32[]{:S(2)}) collective-permute-start(bf16[256,768]{1,0:T(8,128)(2,1)S(1)} %fusion.11), channel_id=1, source_target_pairs={{0,8},{1,9},{2,10},{3,11},{4,12},{5,13},{6,14},{7,15},{8,0},{9,1},... | collective-permute-start | bytes 1179656 | tf_op jit(solution)/shard_map/ppermute | solution.py:29
  443.2 48.2 %collective-permute-start.106 = (bf16[96,2304]{1,0:T(8,128)(2,1)}, bf16[96,2304]{1,0:T(8,128)(2,1)}, u32[]{:S(2)}, u32[]{:S(2)}) collective-permute-start(bf16[96,2304]{1,0:T(8,128)(2,1)} %fusion.9), channel_id=1, source_target_pairs={{0,16},{1,17},{2,18},{3,19},{4,20},{5,21},{6,22},{7,23},{8,24},{9,... | collective-permute-start | bytes 1327112 | tf_op jit(solution)/shard_map/ppermute | solution.py:29
  457.2 35.8 %collective-permute-start.102 = (bf16[96,2304]{1,0:T(8,128)(2,1)}, bf16[96,2304]{1,0:T(8,128)(2,1)}, u32[]{:S(2)}, u32[]{:S(2)}) collective-permute-start(bf16[96,2304]{1,0:T(8,128)(2,1)} %fusion.8), channel_id=1, source_target_pairs={{0,8},{1,9},{2,10},{3,11},{4,12},{5,13},{6,14},{7,15},{8,0},{9,1},... | collective-permute-start | bytes 1327112 | tf_op jit(solution)/shard_map/ppermute | solution.py:29
  497.9 35.2 %collective-permute-start.103 = (bf16[96,2304]{1,0:T(8,128)(2,1)S(1)}, bf16[96,2304]{1,0:T(8,128)(2,1)S(1)}, u32[]{:S(2)}, u32[]{:S(2)}) collective-permute-start(bf16[96,2304]{1,0:T(8,128)(2,1)S(1)} %fusion.1), channel_id=1, source_target_pairs={{0,2},{1,3},{2,0},{3,1},{4,6},{5,7},{6,4},{7,5},{8,10},{9,11},{10,... | collective-permute-start | bytes 1327112 | tf_op jit(solution)/shard_map/ppermute | solution.py:29
  (151 other events, 2225.6 us)
